TPU v7x, 128 devices: a whole 4x4x4 slice. The times are simulated.
128 devices in a mesh: depth: 8 (over z, core), cols: 16 (over x, y).
Axes of the slice: x: 4, y: 4, z: 4, core: 2. Of those that a mesh axis runs over, the one named last changes fastest.
Arguments:
- depth_cell: int32 [8, 16, 16384], P('depth', 'cols'), may hold values from 0 to 15
- column_cell: int32 [8, 16, 16384], P('depth', 'cols'), may hold values from 0 to 263
- row_cell: int32 [8, 16, 16384], P('depth', 'cols'), may hold values from 0 to 127
- mass: bfloat16 [8, 16, 16384], P('depth', 'cols'), may hold values from 2 to 32
- counts: int32 [8, 16], P('depth', 'cols'), may hold values from 1 to 16384, 131072 in all within a row
- diffusion: float32 [3], replicated, may hold values from 0.04 to 0.14
- tf_center: float32 [8], replicated, may hold values from 0.2 to 1.2
- tf_sharp: float32 [8], replicated, may hold values from 1 to 8
- tf_opacity: float32 [8], replicated, may hold values from 0.0015625 to 0.046875
- tf_shade: float32 [8], replicated, may hold values from 0.3 to 3
- tf_color: float32 [8, 3], replicated, may hold values from 0 to 1
Outputs:
- image: float32 [32, 4096, 128], P('depth', 'cols')
Inputs may be any that keep to these rules, and one draw needn't show every extreme that they name: `counts`: some brick of every depth row holds exactly 16384 live particles.
All inputs are finite; a program needn't handle non-finite values. No bound on the sum of `counts` on one device may be relied on, other than what follows from the above.
Results may differ from a plain program's by a relative error of at most 0.0003.
Values sent between devices are 32-bit elements; how exact they have to be, the bound alone decides.
A program may use at most 64 MiB of HBM per device.

v0:
```python
import jax
import jax.numpy as jnp
from jax import lax
from jax.sharding import PartitionSpec as P

CZ = 16
CX = 256
CY = 128
RIM = 4
BLOCK = 2048
SMOOTH = 4
TFS = 8


def passed_along(array, axis, by):
    length = lax.axis_size(axis)
    pairs = [(i, i + by) for i in range(length) if 0 <= i + by < length]
    return lax.ppermute(array, axis, pairs)


def extended_2(cells, sides, width):
    for axis, dim in sides:
        count = lax.axis_size(axis)
        ends = count - 1
        head = lax.slice_in_dim(cells, 0, width, axis=dim)
        tail = lax.slice_in_dim(cells, cells.shape[dim] - width, cells.shape[dim], axis=dim)
        cells = jnp.concatenate(
            [
                lax.ppermute(tail, axis, [(i, (i + 1) % count) for i in range(ends)]),
                cells,
                lax.ppermute(head, axis, [((i + 1) % count, i) for i in range(ends)]),
            ],
            axis=dim,
        )
    return cells


def from_partner(value, axis, distance):
    mask = 2**distance
    pairs = [(source, source ^ mask) for source in range(lax.axis_size(axis))]
    return lax.ppermute(value, axis, pairs)


def smooth_once(density, padded, diffusion):
    along_depth = padded[2:, 1:-1, 1:-1] + padded[:-2, 1:-1, 1:-1] - 2.0 * density
    along_column = padded[1:-1, 2:, 1:-1] + padded[1:-1, :-2, 1:-1] - 2.0 * density
    along_row = padded[1:-1, 1:-1, 2:] + padded[1:-1, 1:-1, :-2] - 2.0 * density
    return (
        density
        + diffusion[0] * along_depth
        + diffusion[1] * along_column
        + diffusion[2] * along_row
    )


def gradient_square(padded):
    slope_depth = (padded[2:, 1:-1, 1:-1] - padded[:-2, 1:-1, 1:-1]) * 0.5
    slope_column = (padded[1:-1, 2:, 1:-1] - padded[1:-1, :-2, 1:-1]) * 0.5
    slope_row = (padded[1:-1, 1:-1, 2:] - padded[1:-1, 1:-1, :-2]) * 0.5
    return slope_depth * slope_depth + slope_column * slope_column + slope_row * slope_row


def render(density, grad_square, center, sharpness, opacity, shade, tint):
    opaque = opacity * jax.nn.sigmoid(sharpness * (density - center))
    log_keep = jnp.log1p(-opaque)
    running_log = jnp.cumsum(log_keep, axis=0)
    weight = jnp.exp(running_log - log_keep) * opaque
    sum_density = jnp.sum(weight * density, axis=0)
    sum_gradient = jnp.sum(weight * grad_square, axis=0)
    colors = tint[:, None, None] * sum_density[None] + shade * sum_gradient[None]
    return jnp.concatenate([colors, jnp.exp(running_log[-1])[None]], axis=0)


def pad_rows(field):
    return jnp.pad(field, ((0, 0), (0, 0), (1, 1)))


def inside_mask(length, margin, first, total):
    global_index = first - margin + jnp.arange(length, dtype=jnp.int32)
    return ((global_index >= 0) & (global_index < total)).astype(jnp.float32)


def composite_pair(front_part, back_part):
    colors = front_part[..., :3, :, :] + front_part[..., 3:4, :, :] * back_part[..., :3, :, :]
    keeping = front_part[..., 3:4, :, :] * back_part[..., 3:4, :, :]
    return jnp.concatenate([colors, keeping], axis=-3)


def shards(
    depth_cell,
    column_cell,
    row_cell,
    mass,
    counts,
    diffusion,
    tf_center,
    tf_sharp,
    tf_opacity,
    tf_shade,
    tf_color,
):
    widest = CX + 2 * RIM
    flat_cell = depth_cell.reshape(-1) * widest + column_cell.reshape(-1)
    row_ids = row_cell.reshape(-1)
    weights = mass.reshape(-1)
    live_count = counts[0, 0]
    flat_columns = jnp.arange(CZ * widest, dtype=jnp.int32)
    row_columns = jnp.arange(CY, dtype=jnp.int32)
    offsets = jnp.arange(BLOCK, dtype=jnp.int32)

    def deposit_block(block_index, running):
        offset = block_index * BLOCK
        cells_here = lax.dynamic_slice_in_dim(flat_cell, offset, BLOCK)
        rows_here = lax.dynamic_slice_in_dim(row_ids, offset, BLOCK)
        mass_here = lax.dynamic_slice_in_dim(weights, offset, BLOCK)
        is_live = offset + offsets < live_count
        weight = jnp.where(is_live, mass_here, jnp.zeros_like(mass_here))
        onehot_cells = jnp.where(
            flat_columns[None, :] == cells_here[:, None],
            weight[:, None],
            jnp.zeros((), jnp.bfloat16),
        )
        onehot_rows = (row_columns[None, :] == rows_here[:, None]).astype(jnp.bfloat16)
        return running + lax.dot_general(
            onehot_cells, onehot_rows, (((0,), (0,)), ((), ())), preferred_element_type=jnp.float32
        )

    block_count = (live_count + BLOCK - 1) // BLOCK
    empty = jnp.zeros((CZ * widest, CY), jnp.float32)
    extended = lax.fori_loop(0, block_count, deposit_block, empty).reshape(CZ, widest, CY)
    from_next = passed_along(extended[:, :RIM], "cols", -1)
    from_prev = passed_along(extended[:, RIM + CX :], "cols", 1)
    density = extended[:, RIM : RIM + CX]
    density = density.at[:, :RIM].add(from_prev)
    density = density.at[:, CX - RIM :].add(from_next)
    margin = SMOOTH + 1
    current = extended_2(density, (("depth", 0), ("cols", 1)), margin)
    depth_first = lax.axis_index("depth") * CZ
    depth_total = lax.axis_size("depth") * CZ
    column_first = lax.axis_index("cols") * CX
    column_total = lax.axis_size("cols") * CX
    for sweep_index in range(SMOOTH):
        margin = margin - 1
        current = smooth_once(current[1:-1, 1:-1, :], pad_rows(current), diffusion)
        depth_mask = inside_mask(current.shape[0], margin, depth_first, depth_total)
        column_mask = inside_mask(current.shape[1], margin, column_first, column_total)
        current = current * depth_mask[:, None, None] * column_mask[None, :, None]
    density = current[1:-1, 1:-1, :]
    grad_square = gradient_square(pad_rows(current))
    pictures = jax.vmap(render, in_axes=(None, None, 0, 0, 0, 0, 0))(
        density, grad_square, tf_center, tf_sharp, tf_opacity, tf_shade, tf_color
    )
    slabs = lax.axis_size("depth")
    per_block = TFS // slabs
    holding = pictures.reshape(slabs, per_block, 4, CX, CY)
    position = lax.axis_index("depth")
    for bit_number in range(slabs.bit_length() - 1):
        bit_value = position >> bit_number & 1
        paired = holding.reshape(holding.shape[0] // 2, 2, per_block, 4, CX, CY)
        kept_part = jnp.where(bit_value == 0, paired[:, 0], paired[:, 1])
        outgoing = jnp.where(bit_value == 0, paired[:, 1], paired[:, 0])
        incoming = from_partner(outgoing, "depth", bit_number)
        front_part = jnp.where(bit_value == 0, kept_part, incoming)
        back_part = jnp.where(bit_value == 0, incoming, kept_part)
        holding = composite_pair(front_part, back_part)
    result = holding.reshape(per_block * 4, CX, CY)
    return result


def solution(mesh):
    placed = (
        P("depth", "cols", None),
        P("depth", "cols", None),
        P("depth", "cols", None),
        P("depth", "cols", None),
        P("depth", "cols"),
        P(),
        P(),
        P(),
        P(),
        P(),
        P(),
    )
    return jax.shard_map(
        shards, mesh=mesh, in_specs=placed, out_specs=P("depth", "cols", None), check_vma=False
    )
```

profile of v0, /device:TPU:6, one launch (start us, length us, event | category | flops | bytes accessed | tf_op | source)
XLA Modules:
  0.0 198.4 jit_solution(12776705434899585270)
XLA Ops:
  2.8 45.7 %while.13 = (s32[]{:T(128)}, f32[4224,128]{1,0:T(8,128)S(1)}, s32[]{:T(128)}, s32[16384]{0:T(1024)S(1)}, s32[]{:T(128)}, /*index=5*/bf16[16384]{0:T(1024)(128)(2...) while((s32[]{:T(128)}, f32[4224,128]{1,0:T(8,128)S(1)}, ...), condition=%wide.region_1.2_spmd.clone, body=%wide.region_0.1_spmd.clone.sunk | while | flops 2232702976 | bytes 4386991 | solution.py:130
  4.2 6.2 %fusion.121 = f32[4224,128]{1,0:T(8,128)S(1)} fusion(f32[4224,128]{1,0:T(8,128)S(1)} %get-tuple-element.202, s32[2048]{0:T(1024)S(1)} %dynamic_slice.17, bf16[2048]{0:T(1024)(128)(2,1)S(1)} %fusion.120, s32[2048]{0:T(1024)S(1)} %dynamic_slice.18), kind=kOutput, calls=%fused_computation.9.clone.1 | convolution fusion | flops 2232696832 | bytes 4345856 | tf_op jit(solution)/shard_map/while/body/dot_general | solution.py:124
  11.8 6.2 %fusion.121 = f32[4224,128]{1,0:T(8,128)S(1)} fusion(f32[4224,128]{1,0:T(8,128)S(1)} %get-tuple-element.202, s32[2048]{0:T(1024)S(1)} %dynamic_slice.17, bf16[2048]{0:T(1024)(128)(2,1)S(1)} %fusion.120, s32[2048]{0:T(1024)S(1)} %dynamic_slice.18), kind=kOutput, calls=%fused_computation.9.clone.1 | convolution fusion | flops 2232696832 | bytes 4345856 | tf_op jit(solution)/shard_map/while/body/dot_general | solution.py:124
  19.5 6.2 %fusion.121 = f32[4224,128]{1,0:T(8,128)S(1)} fusion(f32[4224,128]{1,0:T(8,128)S(1)} %get-tuple-element.202, s32[2048]{0:T(1024)S(1)} %dynamic_slice.17, bf16[2048]{0:T(1024)(128)(2,1)S(1)} %fusion.120, s32[2048]{0:T(1024)S(1)} %dynamic_slice.18), kind=kOutput, calls=%fused_computation.9.clone.1 | convolution fusion | flops 2232696832 | bytes 4345856 | tf_op jit(solution)/shard_map/while/body/dot_general | solution.py:124
  27.1 6.2 %fusion.121 = f32[4224,128]{1,0:T(8,128)S(1)} fusion(f32[4224,128]{1,0:T(8,128)S(1)} %get-tuple-element.202, s32[2048]{0:T(1024)S(1)} %dynamic_slice.17, bf16[2048]{0:T(1024)(128)(2,1)S(1)} %fusion.120, s32[2048]{0:T(1024)S(1)} %dynamic_slice.18), kind=kOutput, calls=%fused_computation.9.clone.1 | convolution fusion | flops 2232696832 | bytes 4345856 | tf_op jit(solution)/shard_map/while/body/dot_general | solution.py:124
  34.7 6.2 %fusion.121 = f32[4224,128]{1,0:T(8,128)S(1)} fusion(f32[4224,128]{1,0:T(8,128)S(1)} %get-tuple-element.202, s32[2048]{0:T(1024)S(1)} %dynamic_slice.17, bf16[2048]{0:T(1024)(128)(2,1)S(1)} %fusion.120, s32[2048]{0:T(1024)S(1)} %dynamic_slice.18), kind=kOutput, calls=%fused_computation.9.clone.1 | convolution fusion | flops 2232696832 | bytes 4345856 | tf_op jit(solution)/shard_map/while/body/dot_general | solution.py:124
  42.3 6.2 %fusion.121 = f32[4224,128]{1,0:T(8,128)S(1)} fusion(f32[4224,128]{1,0:T(8,128)S(1)} %get-tuple-element.202, s32[2048]{0:T(1024)S(1)} %dynamic_slice.17, bf16[2048]{0:T(1024)(128)(2,1)S(1)} %fusion.120, s32[2048]{0:T(1024)S(1)} %dynamic_slice.18), kind=kOutput, calls=%fused_computation.9.clone.1 | convolution fusion | flops 2232696832 | bytes 4345856 | tf_op jit(solution)/shard_map/while/body/dot_general | solution.py:124
  48.6 2.1 %collective-permute-start = (f32[16,4,128]{2,1,0:T(4,128)S(1)}, f32[16,4,128]{2,1,0:T(4,128)S(1)}, u32[]{:S(2)}, u32[]{:S(2)}) collective-permute-start(f32[16,4,128]{2,1,0:T(4,128)S(1)} %get-tuple-element.129), channel_id=1, source_target_pairs={{0,1},{1,2},{2,3},{3,4},{4,5},{5,6},{6,7},{7,8},{8,9},{9,10},{10,1... | collective-permute-start | bytes 98312 | tf_op jit(solution)/shard_map/ppermute | solution.py:18
  50.6 6.0 %collective-permute-start.1 = (f32[16,4,128]{2,1,0:T(4,128)S(1)}, f32[16,4,128]{2,1,0:T(4,128)S(1)}, u32[]{:S(2)}, u32[]{:S(2)}) collective-permute-start(f32[16,4,128]{2,1,0:T(4,128)S(1)} %get-tuple-element.128), channel_id=1, source_target_pairs={{1,0},{2,1},{3,2},{4,3},{5,4},{6,5},{7,6},{8,7},{9,8},{10,9},{11,1... | collective-permute-start | bytes 98312 | tf_op jit(solution)/shard_map/ppermute | solution.py:18
  56.7 1.8 slice.345
  59.6 13.2 %collective-permute-done.1 = f32[16,4,128]{2,1,0:T(4,128)S(1)} collective-permute-done((f32[16,4,128]{2,1,0:T(4,128)S(1)}, f32[16,4,128]{2,1,0:T(4,128)S(1)}, u32[]{:S(2)}, u32[]{:S(2)}) %collective-permute-start.1) | collective-permute-done | bytes 32800 | tf_op jit(solution)/shard_map/ppermute | solution.py:18
  72.9 1.3 collective-permute-start.2
  74.3 1.3 collective-permute-start.3
  76.3 1.9 collective-permute-done.3
  78.3 5.3 %collective-permute-start.4 = (f32[26,5,128]{2,1,0:T(8,128)S(1)}, f32[26,5,128]{2,1,0:T(8,128)S(1)}, u32[]{:S(2)}, u32[]{:S(2)}) collective-permute-start(f32[26,5,128]{2,1,0:T(8,128)S(1)} %get-tuple-element.120), channel_id=1, source_target_pairs={{0,1},{1,2},{2,3},{3,4},{4,5},{5,6},{6,7},{7,8},{8,9},{9,10},{10,1... | collective-permute-start | bytes 199688 | tf_op jit(solution)/shard_map/ppermute | solution.py:29
  83.6 2.8 %collective-permute-start.5 = (f32[26,5,128]{2,1,0:T(8,128)S(1)}, f32[26,5,128]{2,1,0:T(8,128)S(1)}, u32[]{:S(2)}, u32[]{:S(2)}) collective-permute-start(f32[26,5,128]{2,1,0:T(8,128)S(1)} %get-tuple-element.121), channel_id=1, source_target_pairs={{1,0},{2,1},{3,2},{4,3},{5,4},{6,5},{7,6},{8,7},{9,8},{10,9},{11,1... | collective-permute-start | bytes 199688 | tf_op jit(solution)/shard_map/ppermute | solution.py:31
  87.0 3.2 %collective-permute-done.5 = f32[26,5,128]{2,1,0:T(8,128)S(1)} collective-permute-done((f32[26,5,128]{2,1,0:T(8,128)S(1)}, f32[26,5,128]{2,1,0:T(8,128)S(1)}, u32[]{:S(2)}, u32[]{:S(2)}) %collective-permute-start.5) | collective-permute-done | bytes 66592 | tf_op jit(solution)/shard_map/ppermute | solution.py:31
  90.5 5.3 %fusion.30 = f32[24,264,128]{2,1,0:T(8,128)S(1)} fusion(f32[26,266,128]{2,1,0:T(8,128)S(1)} %pad_maximum_fusion, f32[264]{0:T(512)S(1)} %fusion.101, f32[24]{0:T(128)S(1)} %and_convert_fusion.3, f32[]{:T(128)} %bitcast.7, f32[]{:T(128)} %bitcast.6, f32[]{:T(128)} %bitcast.5), kind=kLoop, calls=%fused_computation.45 | loop fusion | flops 12165120 | bytes 23087628 | tf_op jit(solution)/shard_map/mul | solution.py:147
  95.8 5.1 %fusion.42 = f32[22,262,128]{2,1,0:T(8,128)S(1)} fusion(f32[24,264,128]{2,1,0:T(8,128)S(1)} %fusion.30, f32[262]{0:T(512)S(1)} %fusion.103, f32[22]{0:T(128)S(1)} %and_convert_fusion.2, f32[]{:T(128)} %bitcast.7, f32[]{:T(128)} %bitcast.6, f32[]{:T(128)} %bitcast.5), kind=kLoop, calls=%fused_computation.60 | loop fusion | flops 11066880 | bytes 21066252 | tf_op jit(solution)/shard_map/mul | solution.py:147
  100.9 4.6 %fusion.54 = f32[20,260,128]{2,1,0:T(8,128)S(1)} fusion(f32[22,262,128]{2,1,0:T(8,128)S(1)} %fusion.42, f32[260]{0:T(512)S(1)} %fusion.105, f32[20]{0:T(128)S(1)} %and_convert_fusion.1, f32[]{:T(128)} %bitcast.7, f32[]{:T(128)} %bitcast.6, f32[]{:T(128)} %bitcast.5), kind=kLoop, calls=%fused_computation.74 | loop fusion | flops 9984000 | bytes 19155468 | tf_op jit(solution)/shard_map/mul | solution.py:147
  105.5 4.4 %fusion.66 = f32[18,258,128]{2,1,0:T(8,128)S(1)} fusion(f32[20,260,128]{2,1,0:T(8,128)S(1)} %fusion.54, f32[258]{0:T(512)S(1)} %fusion.107, f32[18]{0:T(128)S(1)} %and_convert_fusion, f32[]{:T(128)} %bitcast.7, f32[]{:T(128)} %bitcast.6, f32[]{:T(128)} %bitcast.5), kind=kLoop, calls=%fused_computation.88 | loop fusion | flops 8916480 | bytes 17248780 | tf_op jit(solution)/shard_map/mul | solution.py:147
  109.9 1.7 fusion.77
  111.6 24.2 %multiply_reduce_fusion.1 = (f32[8,256,128]{2,1,0:T(8,128)S(1)}, f32[8,256,128]{2,1,0:T(8,128)S(1)}, f32[8,16,256,128]{3,2,1,0:T(8,128)S(1)}) fusion(f32[16,256,128]{2,1,0:T(8,128)S(1)} %get-tuple-element.127, f32[16,256,128]{2,1,0:T(8,128)S(1)} %get-tuple-element.126, f32[8]{0:T(128)S(1)} %copy-done.5, f32[8]{0:T(128)S(1)} %copy-done.6, f32[8]{0:T(128)S(1)} %copy-done.7), kind=kOutput, calls=%fused_computation.17 | output fusion | flops 146276352 | bytes 23068768 | tf_op jit(solution)/shard_map/vmap(jit(cumsum))/reduce_window_sum | solution.py:66
  136.5 1.6 select_bitcast_fusion
  138.0 7.6 %collective-permute-start.6 = (f32[4,1,4,256,128]{4,3,2,0,1:T(8,128)}, f32[4,1,4,256,128]{4,3,2,0,1:T(8,128)}, u32[]{:S(2)}, u32[]{:S(2)}) collective-permute-start(f32[4,1,4,256,128]{4,3,2,0,1:T(8,128)} %select_bitcast_fusion), channel_id=1, source_target_pairs={{0,16},{16,0},{32,48},{48,32},{64,80},{80,64},{96,112},{112,96},{1... | collective-permute-start | bytes 6291464 | tf_op jit(solution)/shard_map/ppermute | solution.py:41
  145.6 4.1 %collective-permute-done.6 = f32[4,1,4,256,128]{4,3,2,0,1:T(8,128)} collective-permute-done((f32[4,1,4,256,128]{4,3,2,0,1:T(8,128)}, f32[4,1,4,256,128]{4,3,2,0,1:T(8,128)}, u32[]{:S(2)}, u32[]{:S(2)}) %collective-permute-start.6) | collective-permute-done | bytes 2097184 | tf_op jit(solution)/shard_map/ppermute | solution.py:41
  149.7 2.5 %bitcast_select_fusion.1 = (f32[4,1,4,256,128]{4,3,2,0,1:T(8,128)S(1)}, f32[4,1,4,256,128]{4,3,2,0,1:T(8,128)S(1)}) fusion(f32[4,1,4,256,128]{4,3,2,0,1:T(8,128)} %collective-permute-done.6, pred[]{:T(512)S(6)} %eq.34, f32[4,2,1,3,256,128]{5,4,3,0,2,1:T(8,128)S(1)} %multiply_add_fusion, f32[4,2,1,1,256,128]{5,4,1,0,3,2:T(8,128)} %bitcast.76), kind=kLoop, calls=%fused_computation.112 | loop fusion | flops 3670016 | bytes 10486784 | tf_op jit(solution)/shard_map/jit(_where)/select_n | solution.py:163
  152.8 3.4 %collective-permute-start.7 = (f32[2,1,4,256,128]{4,3,2,0,1:T(8,128)S(1)}, f32[2,1,4,256,128]{4,3,2,0,1:T(8,128)}, u32[]{:S(2)}, u32[]{:S(2)}) collective-permute-start(f32[2,1,4,256,128]{4,3,2,0,1:T(8,128)S(1)} %select_bitcast_fusion.1), channel_id=1, source_target_pairs={{0,32},{16,48},{32,0},{48,16},{64,96},{80,112},{96,64},{112,80},{1... | collective-permute-start | bytes 3145736 | tf_op jit(solution)/shard_map/ppermute | solution.py:41
  156.2 23.8 %collective-permute-done.7 = f32[2,1,4,256,128]{4,3,2,0,1:T(8,128)} collective-permute-done((f32[2,1,4,256,128]{4,3,2,0,1:T(8,128)S(1)}, f32[2,1,4,256,128]{4,3,2,0,1:T(8,128)}, u32[]{:S(2)}, u32[]{:S(2)}) %collective-permute-start.7) | collective-permute-done | bytes 1048608 | tf_op jit(solution)/shard_map/ppermute | solution.py:41
  180.0 1.4 broadcast_select_fusion.2
  181.9 3.9 %collective-permute-start.8 = (f32[1,1,4,256,128]{4,3,2,1,0:T(8,128)S(1)}, f32[1,1,4,256,128]{4,3,2,1,0:T(8,128)S(1)}, u32[]{:S(2)}, u32[]{:S(2)}) collective-permute-start(f32[1,1,4,256,128]{4,3,2,1,0:T(8,128)S(1)} %fusion.88), channel_id=1, source_target_pairs={{0,64},{16,80},{32,96},{48,112},{64,0},{80,16},{96,32},{112,48},{1... | collective-permute-start | bytes 1572872 | tf_op jit(solution)/shard_map/ppermute | solution.py:41
  185.8 11.6 %collective-permute-done.8 = f32[1,1,4,256,128]{4,3,2,1,0:T(8,128)S(1)} collective-permute-done((f32[1,1,4,256,128]{4,3,2,1,0:T(8,128)S(1)}, f32[1,1,4,256,128]{4,3,2,1,0:T(8,128)S(1)}, u32[]{:S(2)}, u32[]{:S(2)}) %collective-permute-start.8) | collective-permute-done | bytes 524320 | tf_op jit(solution)/shard_map/ppermute | solution.py:41
  (72 shorter events, 15.7 us)
Async XLA Ops:
  48.5 8.2 %copy-start.1 = (f32[4224,128]{1,0:T(8,128)}, f32[4224,128]{1,0:T(8,128)S(1)}, u32[]{:S(2)}) copy-start(f32[4224,128]{1,0:T(8,128)S(1)} %get-tuple-element.82) | copy-start | bytes 6488068
  48.5 10.0 %copy-start.3 = (f32[8,3]{0,1:T(4,128)S(1)}, f32[8,3]{0,1:T(4,128)}, u32[]{:S(2)}) copy-start(f32[8,3]{0,1:T(4,128)} %param.27) | copy-start | bytes 292
  48.6 10.1 %copy-start.4 = (f32[8]{0:T(128)S(1)}, f32[8]{0:T(128)}, u32[]{:S(2)}) copy-start(f32[8]{0:T(128)} %param.26) | copy-start | bytes 100
  48.6 10.2 %collective-permute-start = (f32[16,4,128]{2,1,0:T(4,128)S(1)}, f32[16,4,128]{2,1,0:T(4,128)S(1)}, u32[]{:S(2)}, u32[]{:S(2)}) collective-permute-start(f32[16,4,128]{2,1,0:T(4,128)S(1)} %get-tuple-element.129), channel_id=1, source_target_pairs={{0,1},{1,2},{2,3},{3,4},{4,5},{5,6},{6,7},{7,8},{8,9},{9,10},{10,1... | collective-permute-start | bytes 98312 | tf_op jit(solution)/shard_map/ppermute | solution.py:18
  50.6 22.2 %collective-permute-start.1 = (f32[16,4,128]{2,1,0:T(4,128)S(1)}, f32[16,4,128]{2,1,0:T(4,128)S(1)}, u32[]{:S(2)}, u32[]{:S(2)}) collective-permute-start(f32[16,4,128]{2,1,0:T(4,128)S(1)} %get-tuple-element.128), channel_id=1, source_target_pairs={{1,0},{2,1},{3,2},{4,3},{5,4},{6,5},{7,6},{8,7},{9,8},{10,9},{11,1... | collective-permute-start | bytes 98312 | tf_op jit(solution)/shard_map/ppermute | solution.py:18
  56.7 18.9 %copy-start.2 = (f32[3]{0:T(128)S(1)}, f32[3]{0:T(128)}, u32[]{:S(2)}) copy-start(f32[3]{0:T(128)} %param.22) | copy-start | bytes 40
  72.9 3.4 %collective-permute-start.2 = (f32[5,256,128]{2,1,0:T(8,128)S(1)}, f32[5,256,128]{2,1,0:T(8,128)S(1)}, u32[]{:S(2)}, u32[]{:S(2)}) collective-permute-start(f32[5,256,128]{2,1,0:T(8,128)S(1)} %get-tuple-element.132), channel_id=1, source_target_pairs={{0,16},{16,32},{32,48},{48,64},{64,80},{80,96},{96,112},{1,17},{17... | collective-permute-start | bytes 1966088 | tf_op jit(solution)/shard_map/ppermute | solution.py:29
  74.3 4.0 %collective-permute-start.3 = (f32[5,256,128]{2,1,0:T(8,128)S(1)}, f32[5,256,128]{2,1,0:T(8,128)S(1)}, u32[]{:S(2)}, u32[]{:S(2)}) collective-permute-start(f32[5,256,128]{2,1,0:T(8,128)S(1)} %get-tuple-element.133), channel_id=1, source_target_pairs={{16,0},{32,16},{48,32},{64,48},{80,64},{96,80},{112,96},{17,1},{33... | collective-permute-start | bytes 1966088 | tf_op jit(solution)/shard_map/ppermute | solution.py:31
  78.3 8.7 %collective-permute-start.4 = (f32[26,5,128]{2,1,0:T(8,128)S(1)}, f32[26,5,128]{2,1,0:T(8,128)S(1)}, u32[]{:S(2)}, u32[]{:S(2)}) collective-permute-start(f32[26,5,128]{2,1,0:T(8,128)S(1)} %get-tuple-element.120), channel_id=1, source_target_pairs={{0,1},{1,2},{2,3},{3,4},{4,5},{5,6},{6,7},{7,8},{8,9},{9,10},{10,1... | collective-permute-start | bytes 199688 | tf_op jit(solution)/shard_map/ppermute | solution.py:29
  83.6 6.6 %collective-permute-start.5 = (f32[26,5,128]{2,1,0:T(8,128)S(1)}, f32[26,5,128]{2,1,0:T(8,128)S(1)}, u32[]{:S(2)}, u32[]{:S(2)}) collective-permute-start(f32[26,5,128]{2,1,0:T(8,128)S(1)} %get-tuple-element.121), channel_id=1, source_target_pairs={{1,0},{2,1},{3,2},{4,3},{5,4},{6,5},{7,6},{8,7},{9,8},{10,9},{11,1... | collective-permute-start | bytes 199688 | tf_op jit(solution)/shard_map/ppermute | solution.py:31
  109.9 1.7 copy-start.5
  109.9 1.7 copy-start.6
  109.9 1.7 copy-start.7
  136.0 2.1 %copy-start = (f32[8,1,256,128]{3,2,1,0:T(8,128)}, f32[8,1,256,128]{3,2,1,0:T(8,128)S(1)}, u32[]{:S(2)}) copy-start(f32[8,1,256,128]{3,2,1,0:T(8,128)S(1)} %slice_exponential_fusion) | copy-start | bytes 3145732
  138.0 11.7 %collective-permute-start.6 = (f32[4,1,4,256,128]{4,3,2,0,1:T(8,128)}, f32[4,1,4,256,128]{4,3,2,0,1:T(8,128)}, u32[]{:S(2)}, u32[]{:S(2)}) collective-permute-start(f32[4,1,4,256,128]{4,3,2,0,1:T(8,128)} %select_bitcast_fusion), channel_id=1, source_target_pairs={{0,16},{16,0},{32,48},{48,32},{64,80},{80,64},{96,112},{112,96},{1... | collective-permute-start | bytes 6291464 | tf_op jit(solution)/shard_map/ppermute | solution.py:41
  152.8 27.2 %collective-permute-start.7 = (f32[2,1,4,256,128]{4,3,2,0,1:T(8,128)S(1)}, f32[2,1,4,256,128]{4,3,2,0,1:T(8,128)}, u32[]{:S(2)}, u32[]{:S(2)}) collective-permute-start(f32[2,1,4,256,128]{4,3,2,0,1:T(8,128)S(1)} %select_bitcast_fusion.1), channel_id=1, source_target_pairs={{0,32},{16,48},{32,0},{48,16},{64,96},{80,112},{96,64},{112,80},{1... | collective-permute-start | bytes 3145736 | tf_op jit(solution)/shard_map/ppermute | solution.py:41
  181.9 15.5 %collective-permute-start.8 = (f32[1,1,4,256,128]{4,3,2,1,0:T(8,128)S(1)}, f32[1,1,4,256,128]{4,3,2,1,0:T(8,128)S(1)}, u32[]{:S(2)}, u32[]{:S(2)}) collective-permute-start(f32[1,1,4,256,128]{4,3,2,1,0:T(8,128)S(1)} %fusion.88), channel_id=1, source_target_pairs={{0,64},{16,80},{32,96},{48,112},{64,0},{80,16},{96,32},{112,48},{1... | collective-permute-start | bytes 1572872 | tf_op jit(solution)/shard_map/ppermute | solution.py:41
where the time goes:
time: 201 us; the launch traced here: 198 us
  other arithmetic  60.3 us (30%)
  waiting for transfers between devices  58.4 us (29%)
  matrix products  37.2 us (19%)
  starting transfers between devices  33.7 us (17%)
  local copies, waits for them, and re-layouts  7.37 us (4%)
    ppermute x3, waiting for transfers between devices, from_partner(): return lax.ppermute(value, axis, pairs)  39.5 us
    dot_general x6, matrix products, deposit_block(): lax.dot_general(onehot_cells, onehot_rows, (((0,), (0,)), ((), ())), pref...  37.2 us
    another operation x1, other arithmetic, render(): running_log = jnp.cumsum(log_keep, axis=0)  24.2 us
    mul x4, other arithmetic, shards(): current = current * depth_mask[:, None, None] * column_mask[None, :, None]  19.3 us
    ppermute x3, starting transfers between devices, from_partner(): return lax.ppermute(value, axis, pairs)  14.8 us
    ppermute x2, waiting for transfers between devices, passed_along(): return lax.ppermute(array, axis, pairs)  13.2 us
    ppermute x2, starting transfers between devices, passed_along(): return lax.ppermute(array, axis, pairs)  8.08 us
    ppermute x2, starting transfers between devices, extended_2(): lax.ppermute(tail, axis, [(i, (i + 1) % count) for i in range(ends)])  6.63 us
  transfers between devices with their start and end apart: 9, of which 7 were waited for; matrix products, arithmetic and copies ran while one was open for 2% of the time, Pallas kernels for 0%

commit v1 on v0

v1 whole, which is shorter than its diff:
```python
import jax, jax.numpy as jnp
from jax import lax
from jax.experimental import pallas as pl
from jax.experimental.pallas import tpu as pltpu
from jax.sharding import PartitionSpec as P

CZ, CX, CY, RIM = 16, 256, 128, 4
SMOOTH, TFS = 4, 8
HALO = SMOOTH + 1
DEEP = CZ + 2 * HALO
PLANE = 288
XO = 16
ROWS = CZ * PLANE
WIN = 64
UNROLL = 8
NBLK = 128

def exchange(x, stride, axis, bit):
    size = x.shape[axis]
    up = pltpu.roll(x, size - stride, axis)
    down = up if 2 * stride == size else pltpu.roll(x, stride, axis)
    return jnp.where(bit, jnp.maximum(x, down), jnp.minimum(x, up))

def bitonic(vs):
    lane = lax.broadcasted_iota(jnp.int32, (8, 128), 1)
    sub = lax.broadcasted_iota(jnp.int32, (8, 128), 0)
    def bit_of(j, i):
        if j < 4:
            return (i >> j) & 1
        if j < 7:
            return (sub >> (j - 4)) & 1
        return (lane >> (j - 7)) & 1
    hot = {j: bit_of(j, 0) == 1 for j in range(4, 14)}
    neg = {j: -bit_of(j, 0) for j in range(4, 14)}
    def flips(j, i):
        if j == 0 or j == 14:
            return 0
        if j < 4:
            return -((i >> j) & 1)
        return neg[j]
    for k in range(1, 15):
        out = []
        for i, v in enumerate(vs):
            a, b = flips(k - 1, i), flips(k, i)
            if isinstance(a, int) and isinstance(b, int):
                v = ~v if a != b else v
            else:
                v = v ^ (a ^ b)
            out.append(v)
        vs = out
        for j in range(k - 1, -1, -1):
            if j < 4:
                out = list(vs)
                for i in range(16):
                    p = i ^ (1 << j)
                    if i < p:
                        out[i] = jnp.minimum(vs[i], vs[p])
                        out[p] = jnp.maximum(vs[i], vs[p])
                vs = out
            elif j < 7:
                vs = [exchange(v, 1 << (j - 4), 0, hot[j]) for v in vs]
            else:
                vs = [exchange(v, 1 << (j - 7), 1, hot[j]) for v in vs]
    return vs

def deposit_kernel(key_ref, out_ref, raw, tidy, ends, sem):
    vs = bitonic([key_ref[8 * i : 8 * i + 8, :] for i in range(16)])
    for i in range(16):
        raw[8 * i : 8 * i + 8, :] = vs[i]
    first = pltpu.make_async_copy(raw.at[pl.ds(0, 8)], ends.at[0], sem.at[0])
    last = pltpu.make_async_copy(raw.at[pl.ds(120, 8)], ends.at[1], sem.at[1])
    first.start()
    last.start()
    tidy[...] = raw[...].T
    zeros = jnp.zeros((PLANE, 128), jnp.float32)

    @pl.loop(0, CZ)
    def _(z):
        out_ref[pl.ds(pl.multiple_of(z * PLANE, 8), PLANE), :] = zeros

    first.wait()
    last.wait()
    ys = lax.broadcasted_iota(jnp.int32, (128, 128), 0)
    ws = lax.broadcasted_iota(jnp.int32, (WIN, 128), 0)

    def window(row, start, y_hot):
        hot = jnp.where(ws == row - start, 1.0, 0.0).astype(jnp.bfloat16)
        return lax.dot_general(hot, y_hot, (((1,), (1,)), ((), ())), preferred_element_type=jnp.float32)

    def y_part(b):
        keys = tidy[pl.ds(b, 1), :]
        mass = (keys & 4095).astype(jnp.float32) * (1.0 / 64.0)
        y = (keys >> 12) & 127
        y_hot = jnp.where(ys == y, mass, 0.0).astype(jnp.bfloat16)
        return (keys >> 19) + 4096, y_hot

    def bounds(b):
        lo = (ends[0, 0, b] >> 19) + 4096
        hi = (ends[1, 7, b] >> 19) + 4096
        start = jnp.minimum((lo >> 3) << 3, ROWS - WIN)
        return pl.multiple_of(start, 8), (hi - start) >> 6

    @pl.loop(0, NBLK // UNROLL)
    def _(g):
        extra = 0
        parts = []
        for u in range(UNROLL):
            b = g * UNROLL + u
            start, more = bounds(b)
            row, y_hot = y_part(b)
            parts.append((start, window(row, start, y_hot)))
            extra = extra + more
        for start, part in parts:
            out_ref[pl.ds(start, WIN), :] += part

        @pl.when(extra > 0)
        def _():
            for u in range(UNROLL):
                b = g * UNROLL + u
                start, more = bounds(b)

                @pl.loop(0, more)
                def _(n):
                    place = pl.multiple_of(jnp.minimum(start + (n + 1) * WIN, ROWS - WIN), 8)
                    skip = start + (n + 1) * WIN - place
                    row, y_hot = y_part(b)
                    row = jnp.where(row - place >= skip, row, -1)
                    out_ref[pl.ds(place, WIN), :] += window(row, place, y_hot)

def keys_of(depth_cell, column_cell, row_cell, mass, count):
    slot = jnp.arange(16384, dtype=jnp.int32)
    weight = jnp.where(slot < count, mass.astype(jnp.float32) * 64.0, 0.0).astype(jnp.int32)
    row = depth_cell * PLANE + column_cell + (XO - RIM) - 4096
    return ((row << 19) | (row_cell << 12) | weight).reshape(128, 128)

def deposit(key):
    return pl.pallas_call(
        deposit_kernel,
        out_shape=jax.ShapeDtypeStruct((ROWS, 128), jnp.float32),
        in_specs=[pl.BlockSpec(memory_space=pltpu.VMEM)],
        out_specs=pl.BlockSpec(memory_space=pltpu.VMEM),
        scratch_shapes=[
            pltpu.VMEM((128, 128), jnp.int32),
            pltpu.VMEM((128, 128), jnp.int32),
            pltpu.SMEM((2, 8, 128), jnp.int32),
            pltpu.SemaphoreType.DMA((2,)),
        ],
        name="deposit",
    )(key)


def lanes_of():
    lane = lax.broadcasted_iota(jnp.int32, (8, 128), 1)
    return jnp.where(lane == 0, 0.0, 1.0), jnp.where(lane == 127, 0.0, 1.0)

def sweep(src, dst, lo, hi, coef, z_live, x_live):
    has_left, has_right = lanes_of()
    center, d0, d1, d2 = coef

    @pl.loop(lo, hi)
    def _(z):
        live = z_live(z)
        c, a, b = center * live, d0 * live, d1 * live
        left, right = has_left * (d2 * live), has_right * (d2 * live)
        for n in range(34):
            r = 8 + 8 * n
            v = src[z, r : r + 8, :]
            along_z = src[z - 1, r : r + 8, :] + src[z + 1, r : r + 8, :]
            along_x = src[z, r - 1 : r + 7, :] + src[z, r + 1 : r + 9, :]
            new = v * c + along_z * a + along_x * b
            new = new + pltpu.roll(v, 1, 1) * left + pltpu.roll(v, 127, 1) * right
            if n == 0:
                new = new * x_live[0]
            if n == 33:
                new = new * x_live[1]
            dst[z, r : r + 8, :] = new

def gradient(src, dst):
    has_left, has_right = lanes_of()
    left, right = has_left * 0.5, has_right * 0.5

    @pl.loop(0, CZ)
    def _(z):
        for n in range(32):
            r = XO + 8 * n
            v = src[z + HALO, r : r + 8, :]
            gz = (src[z + HALO + 1, r : r + 8, :] - src[z + HALO - 1, r : r + 8, :]) * 0.5
            gx = (src[z + HALO, r + 1 : r + 9, :] - src[z + HALO, r - 1 : r + 7, :]) * 0.5
            gy = pltpu.roll(v, 127, 1) * right - pltpu.roll(v, 1, 1) * left
            dst[z, 8 * n : 8 * n + 8, :] = gz * gz + gx * gx + gy * gy

def render(dens, grad, out, tf_ref, functions):
    @pl.loop(0, CX // 8)
    def _(n):
        r = pl.multiple_of(8 * n, 8)
        keep = {k: jnp.ones((8, 128), jnp.float32) for k in functions}
        sums = {k: None for k in functions}
        for z in range(CZ):
            d = dens[z + HALO, pl.ds(r + XO, 8), :]
            g = grad[z, pl.ds(r, 8), :]
            for k in functions:
                t = jnp.tanh(d * tf_ref[0, k] + tf_ref[1, k])
                opaque = t * tf_ref[2, k] + tf_ref[2, k]
                w = keep[k] * opaque
                keep[k] = keep[k] - w
                if sums[k] is None:
                    sums[k] = (w * d, w * g)
                else:
                    sums[k] = (sums[k][0] + w * d, sums[k][1] + w * g)
        for k in functions:
            out[k, 0, pl.ds(r, 8), :] = sums[k][0]
            out[k, 1, pl.ds(r, 8), :] = sums[k][1]
            out[k, 2, pl.ds(r, 8), :] = keep[k]

def local_kernel(par_ref, tf_ref, low, mid, high, out, one, two, grad, sem):
    copies = [
        pltpu.make_async_copy(mid, one.at[pl.ds(HALO, CZ)], sem.at[0]),
        pltpu.make_async_copy(low, one.at[pl.ds(0, HALO)], sem.at[1]),
        pltpu.make_async_copy(high, one.at[pl.ds(HALO + CZ, HALO)], sem.at[2]),
    ]
    for copy in copies:
        copy.start()
    x_live = (par_ref[4], par_ref[5])
    coef = tuple(par_ref[i] for i in range(4))
    zeros = jnp.zeros((8, 128), jnp.float32)

    @pl.loop(0, DEEP)
    def _(z):
        two[z, 0:8, :] = zeros
        two[z, 280:288, :] = zeros
    for copy in copies:
        copy.wait()

    @pl.loop(0, DEEP)
    def _(z):
        one[z, 8:16, :] = one[z, 8:16, :] * x_live[0]
        one[z, 272:280, :] = one[z, 272:280, :] * x_live[1]

    def z_live(z):
        return jnp.where(z < HALO, par_ref[6], jnp.where(z >= HALO + CZ, par_ref[7], 1.0))

    src, dst = one, two
    for s in range(SMOOTH):
        sweep(src, dst, s + 1, DEEP - s - 1, coef, z_live, x_live)
        src, dst = dst, src
    gradient(src, grad)
    render(src, grad, out, tf_ref, range(TFS))

def local(par, tf, low, mid, high):
    smem = pl.BlockSpec(memory_space=pltpu.SMEM)
    any_ = pl.BlockSpec(memory_space=pl.ANY)
    return pl.pallas_call(
        local_kernel,
        out_shape=jax.ShapeDtypeStruct((TFS, 3, CX, CY), jnp.float32),
        in_specs=[smem, smem, any_, any_, any_],
        out_specs=pl.BlockSpec(memory_space=pltpu.VMEM),
        scratch_shapes=[
            pltpu.VMEM((DEEP, PLANE, CY), jnp.float32),
            pltpu.VMEM((DEEP, PLANE, CY), jnp.float32),
            pltpu.VMEM((CZ, CX, CY), jnp.float32),
            pltpu.SemaphoreType.DMA((3,)),
        ],
        compiler_params=pltpu.CompilerParams(vmem_limit_bytes=48 << 20),
        name="local",
    )(par, tf, low, mid, high)


def passed_along(array, axis, by):
    length = lax.axis_size(axis)
    pairs = [(i, i + by) for i in range(length) if 0 <= i + by < length]
    return lax.ppermute(array, axis, pairs)


def from_partner(value, axis, distance):
    pairs = [(source, source ^ distance) for source in range(lax.axis_size(axis))]
    return lax.ppermute(value, axis, pairs)


def shards(depth_cell, column_cell, row_cell, mass, counts, diffusion, tf_center, tf_sharp, tf_opacity, tf_shade, tf_color):
    key = keys_of(
        depth_cell.reshape(-1), column_cell.reshape(-1), row_cell.reshape(-1), mass.reshape(-1), counts[0, 0]
    )
    extended = deposit(key).reshape(CZ, PLANE, CY)
    from_prev = passed_along(extended[:, 264:280], "cols", 1)
    from_next = passed_along(extended[:, 8:24], "cols", -1)
    extended = extended.at[:, 8:24].add(from_prev).at[:, 264:280].add(from_next)
    low = passed_along(extended[CZ - HALO :], "depth", 1)
    high = passed_along(extended[:HALO], "depth", -1)
    depth, cols = lax.axis_index("depth"), lax.axis_index("cols")
    lives = jnp.stack(
        [cols > 0, cols < lax.axis_size("cols") - 1, depth > 0, depth < lax.axis_size("depth") - 1]
    ).astype(jnp.float32)
    par = jnp.concatenate([1.0 - 2.0 * jnp.sum(diffusion, keepdims=True), diffusion, lives])
    tf = jnp.stack([0.5 * tf_sharp, -0.5 * tf_sharp * tf_center, 0.5 * tf_opacity])
    holding = local(par, tf, low, extended, high)
    for bit in (1, 2, 4):
        upper = (depth & bit) != 0
        half = holding.shape[0] // 2
        pairs = holding.reshape(half, 2, 3, CX, CY)
        kept = jnp.where(upper, pairs[:, 1], pairs[:, 0])
        sent = jnp.where(upper, pairs[:, 0], pairs[:, 1])
        came = from_partner(sent, "depth", bit)
        front, back = jnp.where(upper, came, kept), jnp.where(upper, kept, came)
        through = front[:, 2:]
        holding = jnp.concatenate([front[:, :2] + through * back[:, :2], through * back[:, 2:]], axis=1)
    dens, grad, keep = holding[0]
    tint = lax.dynamic_slice_in_dim(tf_color, depth, 1)[0]
    shade = lax.dynamic_slice_in_dim(tf_shade, depth, 1)
    colors = tint[:, None, None] * dens + shade[:, None, None] * grad
    return jnp.concatenate([colors, keep[None]], axis=0)


def solution(mesh):
    brick = P("depth", "cols", None)
    placed = (brick,) * 4 + (P("depth", "cols"),) + (P(),) * 6
    return jax.shard_map(shards, mesh=mesh, in_specs=placed, out_specs=brick, check_vma=False)
```

time: 201 us -> 122 us (0.61); the launches traced: 198 us -> 122 us
  other arithmetic: 60.3 us -> 14.4 us
  matrix products: 37.2 us -> 0 us
  Pallas kernels: 0 us -> 35.3 us
  waiting for transfers between devices: 58.4 us -> 43.3 us
  starting transfers between devices: 33.7 us -> 23.7 us
  local copies, waits for them, and re-layouts: 7.37 us -> 3.31 us
    dot_general x6 -> x0, matrix products: 37.2 us -> none  [deposit_block(): lax.dot_general(onehot_cells, onehot_rows, (((0,), (0,)), ((), ())), pref...]
    pallas_call x0 -> x2, Pallas kernels: none -> 35.3 us  [the longest x1 24 us: local(): pl.pallas_call(local_kernel, out_shape=jax.ShapeDtypeStruct((TFS, 3, CX,...]
    another operation x1 -> x4, other arithmetic: 24.2 us -> 1.6 us  [render(): running_log = jnp.cumsum(log_keep, axis=0)]
    mul x7 -> x5, other arithmetic: 19.5 us -> 1.72 us  [the longest x1 0.92 us: keys_of(): mass.astype(jnp.float32) * 64.0]
    ppermute x4 -> x0, starting transfers between devices: 10.8 us -> none  [the longest x2 6.63 us: extended_2(): lax.ppermute(tail, axis, [(i, (i + 1) % count) for i in range(ends)])]
    ppermute x3, waiting for transfers between devices: 39.5 us -> 29.6 us  [from_partner(): return lax.ppermute(value, axis, pairs)]
    ppermute x4 -> x0, waiting for transfers between devices: 5.68 us -> none  [the longest x2 5.14 us: extended_2(): lax.ppermute(head, axis, [((i + 1) % count, i) for i in range(ends)])]
    select_n x12 -> x6, other arithmetic: 9.7 us -> 5.61 us  [the longest x3 3.55 us: shards(): sent = jnp.where(upper, pairs[:, 0], pairs[:, 1])]
  transfers between devices with their start and end apart: 9 -> 7, of which waited for: 7 -> 7; matrix products, arithmetic and copies ran while one was open for 2% -> 1% of each run, Pallas kernels for 0% -> 0%
where the time goes in v1:
time: 122 us
  waiting for transfers between devices  43.3 us (35%)
  Pallas kernels  35.3 us (29%)
  starting transfers between devices  23.7 us (19%)
  other arithmetic  14.4 us (12%)
  local copies, waits for them, and re-layouts  3.31 us (3%)
  between operations  1.57 us (1%)
    ppermute x3, waiting for transfers between devices, from_partner(): return lax.ppermute(value, axis, pairs)  29.6 us
    pallas_call x1, Pallas kernels, local(): pl.pallas_call(local_kernel, out_shape=jax.ShapeDtypeStruct((TFS, 3, CX,...  24 us
    ppermute x3, starting transfers between devices, from_partner(): return lax.ppermute(value, axis, pairs)  15.7 us
    ppermute x4, waiting for transfers between devices, passed_along(): return lax.ppermute(array, axis, pairs)  13.7 us
    pallas_call x1, Pallas kernels, deposit(): pl.pallas_call(deposit_kernel, out_shape=jax.ShapeDtypeStruct((ROWS, 128)...  11.3 us
    ppermute x4, starting transfers between devices, passed_along(): return lax.ppermute(array, axis, pairs)  8.02 us
    select_n x3, other arithmetic, shards(): sent = jnp.where(upper, pairs[:, 0], pairs[:, 1])  3.55 us
  transfers between devices with their start and end apart: 7, of which 7 were waited for; matrix products, arithmetic and copies ran while one was open for 1% of the time, Pallas kernels for 0%

profile of v1, /device:TPU:6, one launch (start us, length us, event | category | flops | bytes accessed | tf_op | source)
XLA Modules:
  0.0 121.6 jit_solution(15849200887823678748)
XLA Ops:
  0.0 0.9 convert_multiply_fusion
  1.6 1.0 shift-left_or_fusion
  2.6 0.7 convert_or_fusion.key_ref
  3.3 11.3 %deposit.1 = f32[4608,128]{1,0:T(8,128)} custom-call(s32[128,128]{1,0:T(8,128)} %convert_or_fusion.key_ref), custom_call_target="tpu_custom_call" | custom-call | tf_op jit(solution)/shard_map/deposit/pallas_call | solution.py:137
  14.5 0.9 slice.147
  15.5 2.8 %collective-permute-start = (f32[16,16,128]{2,1,0:T(8,128)S(1)}, f32[16,16,128]{2,1,0:T(8,128)S(1)}, u32[]{:S(2)}, u32[]{:S(2)}) collective-permute-start(f32[16,16,128]{2,1,0:T(8,128)S(1)} %slice.147), channel_id=1, source_target_pairs={{0,1},{1,2},{2,3},{3,4},{4,5},{5,6},{6,7},{7,8},{8,9},{9,10},{10,1... | collective-permute-start | bytes 393224 | tf_op jit(solution)/shard_map/ppermute | solution.py:271
  18.2 6.2 %collective-permute-done = f32[16,16,128]{2,1,0:T(8,128)S(1)} collective-permute-done((f32[16,16,128]{2,1,0:T(8,128)S(1)}, f32[16,16,128]{2,1,0:T(8,128)S(1)}, u32[]{:S(2)}, u32[]{:S(2)}) %collective-permute-start) | collective-permute-done | bytes 131104 | tf_op jit(solution)/shard_map/ppermute | solution.py:271
  24.4 1.6 %fusion.9 = (f32[16,16,128]{2,1,0:T(8,128)S(1)}, f32[16,288,128]{2,1,0:T(8,128)}) fusion(f32[16,288,128]{2,1,0:T(8,128)} %bitcast.83, f32[16,16,128]{2,1,0:T(8,128)S(1)} %collective-permute-done), kind=kLoop, calls=%fused_computation.50 | loop fusion | flops 32768 | bytes 524288 | tf_op jit(solution)/shard_map/slice.75
  26.0 2.6 %collective-permute-start.1 = (f32[16,16,128]{2,1,0:T(8,128)S(1)}, f32[16,16,128]{2,1,0:T(8,128)S(1)}, u32[]{:S(2)}, u32[]{:S(2)}) collective-permute-start(f32[16,16,128]{2,1,0:T(8,128)S(1)} %get-tuple-element.35), channel_id=1, source_target_pairs={{1,0},{2,1},{3,2},{4,3},{5,4},{6,5},{7,6},{8,7},{9,8},{10,9},{11,1... | collective-permute-start | bytes 393224 | tf_op jit(solution)/shard_map/ppermute | solution.py:271
  28.7 0.7 reduce_sum.9
  30.1 2.8 %collective-permute-done.1 = f32[16,16,128]{2,1,0:T(8,128)S(1)} collective-permute-done((f32[16,16,128]{2,1,0:T(8,128)S(1)}, f32[16,16,128]{2,1,0:T(8,128)S(1)}, u32[]{:S(2)}, u32[]{:S(2)}) %collective-permute-start.1) | collective-permute-done | bytes 131104 | tf_op jit(solution)/shard_map/ppermute | solution.py:271
  32.9 1.6 %fusion.7.mid = f32[16,288,128]{2,1,0:T(8,128)} fusion(f32[16,288,128]{2,1,0:T(8,128)} %get-tuple-element.36, f32[16,16,128]{2,1,0:T(8,128)S(1)} %collective-permute-done.1), kind=kLoop, calls=%fused_computation.35 | loop fusion | flops 32768 | bytes 393216 | tf_op jit(solution)/shard_map/scatter-add | solution.py:286
  34.5 1.6 %fusion.8 = (f32[5,288,128]{2,1,0:T(8,128)S(1)}, f32[5,288,128]{2,1,0:T(8,128)S(1)}) fusion(f32[16,288,128]{2,1,0:T(8,128)} %fusion.7.mid), kind=kLoop, calls=%fused_computation.49 | loop fusion | bytes 2949120 | tf_op jit(solution)/shard_map/slice | solution.py:288
  36.1 1.3 %collective-permute-start.2 = (f32[5,288,128]{2,1,0:T(8,128)S(1)}, f32[5,288,128]{2,1,0:T(8,128)S(1)}, u32[]{:S(2)}, u32[]{:S(2)}) collective-permute-start(f32[5,288,128]{2,1,0:T(8,128)S(1)} %get-tuple-element.34), channel_id=1, source_target_pairs={{0,16},{16,32},{32,48},{48,64},{64,80},{80,96},{96,112},{1,17},{17... | collective-permute-start | bytes 2211848 | tf_op jit(solution)/shard_map/ppermute | solution.py:271
  37.4 1.3 %collective-permute-start.3 = (f32[5,288,128]{2,1,0:T(8,128)S(1)}, f32[5,288,128]{2,1,0:T(8,128)S(1)}, u32[]{:S(2)}, u32[]{:S(2)}) collective-permute-start(f32[5,288,128]{2,1,0:T(8,128)S(1)} %get-tuple-element.33), channel_id=1, source_target_pairs={{16,0},{32,16},{48,32},{64,48},{80,64},{96,80},{112,96},{17,1},{33... | collective-permute-start | bytes 2211848 | tf_op jit(solution)/shard_map/ppermute | solution.py:271
  38.9 0.3 collective-permute-done.2.low
  39.2 4.5 %collective-permute-done.3.high = f32[5,288,128]{2,1,0:T(8,128)S(1)} collective-permute-done((f32[5,288,128]{2,1,0:T(8,128)S(1)}, f32[5,288,128]{2,1,0:T(8,128)S(1)}, u32[]{:S(2)}, u32[]{:S(2)}) %collective-permute-start.3) | collective-permute-done | bytes 737312 | tf_op jit(solution)/shard_map/ppermute | solution.py:271
  43.7 24.0 %local.1 = f32[8,3,256,128]{3,2,1,0:T(8,128)} custom-call(f32[8]{0:T(128)S(1)} %pad_maximum_fusion.3.par_ref, f32[3,8]{1,0:T(4,128)S(1)} %pad_maximum_fusion.2.tf_ref, f32[5,288,128]{2,1,0:T(8,128)S(1)} %collective-permute-done.2.low, f32[16,288,128]{2,1,0:T(8,128)S(1)} %copy-done.1, f32[5,288,128]{2,1,0:T(8,128)S(1)} %collective-permute-done.3.high), custom_call_target="tpu_custom_call" | custom-call | tf_op jit(solution)/shard_map/local/pallas_call | solution.py:252
  67.7 3.4 %select_bitcast_fusion = f32[4,3,256,128]{3,2,1,0:T(8,128)} fusion(f32[4,2,3,256,128]{4,3,2,1,0:T(8,128)} %bitcast.84, pred[]{:T(512)S(6)} %ne.11), kind=kLoop, calls=%fused_computation.5 | loop fusion | flops 393216 | bytes 4718593 | tf_op jit(solution)/shard_map/jit(_where)/select_n | solution.py:301
  71.1 9.2 %collective-permute-start.4 = (f32[4,3,256,128]{3,2,1,0:T(8,128)}, f32[4,3,256,128]{3,2,1,0:T(8,128)}, u32[]{:S(2)}, u32[]{:S(2)}) collective-permute-start(f32[4,3,256,128]{3,2,1,0:T(8,128)} %select_bitcast_fusion), channel_id=1, source_target_pairs={{0,16},{16,0},{32,48},{48,32},{64,80},{80,64},{96,112},{112,96},{1... | collective-permute-start | bytes 4718600 | tf_op jit(solution)/shard_map/ppermute | solution.py:276
  80.3 3.4 %collective-permute-done.4 = f32[4,3,256,128]{3,2,1,0:T(8,128)} collective-permute-done((f32[4,3,256,128]{3,2,1,0:T(8,128)}, f32[4,3,256,128]{3,2,1,0:T(8,128)}, u32[]{:S(2)}, u32[]{:S(2)}) %collective-permute-start.4) | collective-permute-done | bytes 1572896 | tf_op jit(solution)/shard_map/ppermute | solution.py:276
  83.7 1.9 %bitcast_select_fusion.1 = (f32[4,3,256,128]{3,2,1,0:T(8,128)S(1)}, f32[4,3,256,128]{3,2,1,0:T(8,128)S(1)}) fusion(f32[4,3,256,128]{3,2,1,0:T(8,128)} %collective-permute-done.4, pred[]{:T(512)S(6)} %ne.11, f32[4,2,3,256,128]{4,3,2,1,0:T(8,128)S(1)} %bitcast.85), kind=kLoop, calls=%fused_computation.4 | loop fusion | flops 1179648 | bytes 7865344 | tf_op jit(solution)/shard_map/jit(_where)/select_n | solution.py:303
  85.6 0.2 fusion.1
  86.0 1.8 %collective-permute-start.5 = (f32[2,3,256,128]{3,2,1,0:T(8,128)S(1)}, f32[2,3,256,128]{3,2,1,0:T(8,128)S(1)}, u32[]{:S(2)}, u32[]{:S(2)}) collective-permute-start(f32[2,3,256,128]{3,2,1,0:T(8,128)S(1)} %fusion.2), channel_id=1, source_target_pairs={{0,32},{16,48},{32,0},{48,16},{64,96},{80,112},{96,64},{112,80},{1... | collective-permute-start | bytes 2359304 | tf_op jit(solution)/shard_map/ppermute | solution.py:276
  87.7 18.1 %collective-permute-done.5 = f32[2,3,256,128]{3,2,1,0:T(8,128)S(1)} collective-permute-done((f32[2,3,256,128]{3,2,1,0:T(8,128)S(1)}, f32[2,3,256,128]{3,2,1,0:T(8,128)S(1)}, u32[]{:S(2)}, u32[]{:S(2)}) %collective-permute-start.5) | collective-permute-done | bytes 786464 | tf_op jit(solution)/shard_map/ppermute | solution.py:276
  105.9 0.1 bitcast_select_fusion.4
  106.3 4.8 %collective-permute-start.6 = (f32[1,3,256,128]{3,2,1,0:T(8,128)S(1)}, f32[1,3,256,128]{3,2,1,0:T(8,128)S(1)}, u32[]{:S(2)}, u32[]{:S(2)}) collective-permute-start(f32[1,3,256,128]{3,2,1,0:T(8,128)S(1)} %select_bitcast_fusion.1), channel_id=1, source_target_pairs={{0,64},{16,80},{32,96},{48,112},{64,0},{80,16},{96,32},{112,48},{1... | collective-permute-start | bytes 1179656 | tf_op jit(solution)/shard_map/ppermute | solution.py:276
  111.1 0.6 dynamic_slice.7
  111.7 0.2 dynamic-slice_reduce_fusion
  111.8 8.0 %collective-permute-done.6 = f32[1,3,256,128]{3,2,1,0:T(8,128)S(1)} collective-permute-done((f32[1,3,256,128]{3,2,1,0:T(8,128)S(1)}, f32[1,3,256,128]{3,2,1,0:T(8,128)S(1)}, u32[]{:S(2)}, u32[]{:S(2)}) %collective-permute-start.6) | collective-permute-done | bytes 393248 | tf_op jit(solution)/shard_map/ppermute | solution.py:276
  120.0 0.7 slice_bitcast_fusion.4
  120.8 0.8 pad_maximum_fusion.1
  (32 shorter events, 0.9 us)
Async XLA Ops:
  0.0 111.7 %copy-start = (f32[8,3]{0,1:T(4,128)S(1)}, f32[8,3]{0,1:T(4,128)}, u32[]{:S(2)}) copy-start(f32[8,3]{0,1:T(4,128)} %param.25) | copy-start | bytes 292
  3.3 25.4 %copy-start.3 = (f32[3]{0:T(128)S(1)}, f32[3]{0:T(128)}, u32[]{:S(2)}) copy-start(f32[3]{0:T(128)} %param.20) | copy-start | bytes 40
  15.5 9.0 %collective-permute-start = (f32[16,16,128]{2,1,0:T(8,128)S(1)}, f32[16,16,128]{2,1,0:T(8,128)S(1)}, u32[]{:S(2)}, u32[]{:S(2)}) collective-permute-start(f32[16,16,128]{2,1,0:T(8,128)S(1)} %slice.147), channel_id=1, source_target_pairs={{0,1},{1,2},{2,3},{3,4},{4,5},{5,6},{6,7},{7,8},{8,9},{9,10},{10,1... | collective-permute-start | bytes 393224 | tf_op jit(solution)/shard_map/ppermute | solution.py:271
  26.0 6.8 %collective-permute-start.1 = (f32[16,16,128]{2,1,0:T(8,128)S(1)}, f32[16,16,128]{2,1,0:T(8,128)S(1)}, u32[]{:S(2)}, u32[]{:S(2)}) collective-permute-start(f32[16,16,128]{2,1,0:T(8,128)S(1)} %get-tuple-element.35), channel_id=1, source_target_pairs={{1,0},{2,1},{3,2},{4,3},{5,4},{6,5},{7,6},{8,7},{9,8},{10,9},{11,1... | collective-permute-start | bytes 393224 | tf_op jit(solution)/shard_map/ppermute | solution.py:271
  34.5 4.4 %copy-start.6 = (f32[8]{0:T(128)S(1)}, f32[8]{0:T(128)}, u32[]{:S(2)}) copy-start(f32[8]{0:T(128)} %param.23) | copy-start | bytes 100
  34.5 4.4 %copy-start.4 = (f32[8]{0:T(128)S(1)}, f32[8]{0:T(128)}, u32[]{:S(2)}) copy-start(f32[8]{0:T(128)} %param.22) | copy-start | bytes 100
  34.5 4.4 %copy-start.5 = (f32[8]{0:T(128)S(1)}, f32[8]{0:T(128)}, u32[]{:S(2)}) copy-start(f32[8]{0:T(128)} %param.21) | copy-start | bytes 100
  34.5 9.2 %copy-start.1 = (f32[16,288,128]{2,1,0:T(8,128)S(1)}, f32[16,288,128]{2,1,0:T(8,128)}, u32[]{:S(2)}) copy-start(f32[16,288,128]{2,1,0:T(8,128)} %fusion.7.mid) | copy-start | bytes 7077892
  36.1 3.1 %collective-permute-start.2 = (f32[5,288,128]{2,1,0:T(8,128)S(1)}, f32[5,288,128]{2,1,0:T(8,128)S(1)}, u32[]{:S(2)}, u32[]{:S(2)}) collective-permute-start(f32[5,288,128]{2,1,0:T(8,128)S(1)} %get-tuple-element.34), channel_id=1, source_target_pairs={{0,16},{16,32},{32,48},{48,64},{64,80},{80,96},{96,112},{1,17},{17... | collective-permute-start | bytes 2211848 | tf_op jit(solution)/shard_map/ppermute | solution.py:271
  37.4 6.2 %collective-permute-start.3 = (f32[5,288,128]{2,1,0:T(8,128)S(1)}, f32[5,288,128]{2,1,0:T(8,128)S(1)}, u32[]{:S(2)}, u32[]{:S(2)}) collective-permute-start(f32[5,288,128]{2,1,0:T(8,128)S(1)} %get-tuple-element.33), channel_id=1, source_target_pairs={{16,0},{32,16},{48,32},{64,48},{80,64},{96,80},{112,96},{17,1},{33... | collective-permute-start | bytes 2211848 | tf_op jit(solution)/shard_map/ppermute | solution.py:271
  67.7 16.0 %copy-start.2 = (f32[8,3,256,128]{3,2,1,0:T(8,128)S(1)}, f32[8,3,256,128]{3,2,1,0:T(8,128)}, u32[]{:S(2)}) copy-start(f32[8,3,256,128]{3,2,1,0:T(8,128)} %local.1) | copy-start | bytes 9437188
  71.1 12.6 %collective-permute-start.4 = (f32[4,3,256,128]{3,2,1,0:T(8,128)}, f32[4,3,256,128]{3,2,1,0:T(8,128)}, u32[]{:S(2)}, u32[]{:S(2)}) collective-permute-start(f32[4,3,256,128]{3,2,1,0:T(8,128)} %select_bitcast_fusion), channel_id=1, source_target_pairs={{0,16},{16,0},{32,48},{48,32},{64,80},{80,64},{96,112},{112,96},{1... | collective-permute-start | bytes 4718600 | tf_op jit(solution)/shard_map/ppermute | solution.py:276
  86.0 19.9 %collective-permute-start.5 = (f32[2,3,256,128]{3,2,1,0:T(8,128)S(1)}, f32[2,3,256,128]{3,2,1,0:T(8,128)S(1)}, u32[]{:S(2)}, u32[]{:S(2)}) collective-permute-start(f32[2,3,256,128]{3,2,1,0:T(8,128)S(1)} %fusion.2), channel_id=1, source_target_pairs={{0,32},{16,48},{32,0},{48,16},{64,96},{80,112},{96,64},{112,80},{1... | collective-permute-start | bytes 2359304 | tf_op jit(solution)/shard_map/ppermute | solution.py:276
  106.1 4.9 %copy-start.7 = (f32[8]{0:T(128)S(1)}, f32[8]{0:T(128)}, u32[]{:S(2)}) copy-start(f32[8]{0:T(128)} %param.24) | copy-start | bytes 100
  106.3 13.6 %collective-permute-start.6 = (f32[1,3,256,128]{3,2,1,0:T(8,128)S(1)}, f32[1,3,256,128]{3,2,1,0:T(8,128)S(1)}, u32[]{:S(2)}, u32[]{:S(2)}) collective-permute-start(f32[1,3,256,128]{3,2,1,0:T(8,128)S(1)} %select_bitcast_fusion.1), channel_id=1, source_target_pairs={{0,64},{16,80},{32,96},{48,112},{64,0},{80,16},{96,32},{112,48},{1... | collective-permute-start | bytes 1179656 | tf_op jit(solution)/shard_map/ppermute | solution.py:276

commit v2 on v1

v2 whole, which is shorter than its diff:
```python
import functools

import jax
import jax.numpy as jnp
import numpy as np
from jax import lax
from jax.experimental import pallas as pl
from jax.experimental.pallas import tpu as pltpu
from jax.sharding import PartitionSpec as P

CZ, CX, CY, RIM = 16, 256, 128, 4
SMOOTH, TFS = 4, 8
HALO = SMOOTH + 1
DEEP = CZ + 2 * HALO
PLANE = 288
XO = 16
ROWS = CZ * PLANE
WIN = 64
UNROLL = 8
SLOTS = 16384
NBLK = SLOTS // 128
MESH = pl.DeviceIdType.MESH
F32, BF16 = jnp.float32, jnp.bfloat16


def split(matrix):
    top = matrix.astype(BF16)
    return top, (matrix - top.astype(np.float64)).astype(BF16)


def tables():
    n = np.arange(1, CY + 1, dtype=np.float64)
    sine = np.sqrt(2.0 / (CY + 1)) * np.sin(np.pi * np.outer(n, n) / (CY + 1))
    slope = 0.5 * (np.eye(CY, k=-1) - np.eye(CY, k=1))
    s_top, s_low = split(sine)
    b_top, b_low = split(np.concatenate([sine, sine @ slope], axis=1))
    cosine = np.broadcast_to(2.0 * np.cos(np.pi * n / (CY + 1)), (8, CY)).astype(np.float32)
    return np.concatenate([s_top, s_top]), s_low, np.concatenate([b_top, b_top]), b_low, cosine


def apply(value, both, low):
    top = value.astype(BF16)
    rest = (value - top.astype(F32)).astype(BF16)
    return jnp.dot(jnp.concatenate([top, rest], axis=1), both, preferred_element_type=F32) + jnp.dot(
        top, low, preferred_element_type=F32
    )


def exchange(x, stride, axis, bit):
    size = x.shape[axis]
    up = pltpu.roll(x, size - stride, axis)
    down = up if 2 * stride == size else pltpu.roll(x, stride, axis)
    return jnp.where(bit, jnp.maximum(x, down), jnp.minimum(x, up))


def bitonic(vs):
    lane = lax.broadcasted_iota(jnp.int32, (8, 128), 1)
    sub = lax.broadcasted_iota(jnp.int32, (8, 128), 0)
    bits = {j: (sub >> (j - 4)) & 1 if j < 7 else (lane >> (j - 7)) & 1 for j in range(4, 14)}
    hot = {j: bits[j] == 1 for j in bits}
    neg = {j: -bits[j] for j in bits}

    def flips(j, i):
        if j == 0 or j == 14:
            return 0
        return -((i >> j) & 1) if j < 4 else neg[j]

    for k in range(1, 15):
        out = []
        for i, v in enumerate(vs):
            a, b = flips(k - 1, i), flips(k, i)
            if isinstance(a, int) and isinstance(b, int):
                out.append(~v if a != b else v)
            else:
                out.append(v ^ (a ^ b))
        vs = out
        for j in range(k - 1, -1, -1):
            if j >= 7:
                vs = [exchange(v, 1 << (j - 7), 1, hot[j]) for v in vs]
            elif j >= 4:
                vs = [exchange(v, 1 << (j - 4), 0, hot[j]) for v in vs]
            else:
                out = list(vs)
                for i in range(16):
                    p = i ^ (1 << j)
                    if i < p:
                        out[i] = jnp.minimum(vs[i], vs[p])
                        out[p] = jnp.maximum(vs[i], vs[p])
                vs = out
    return vs


def deposit_kernel(count, zc, xc, yc, mass, both, low, out, acc, wide, raw, tidy, ends, sem):
    for i in range(128):
        wide[i : i + 1, :] = mass[0, 0:1, 128 * i : 128 * i + 128].astype(F32)
    slot = 128 * lax.broadcasted_iota(jnp.int32, (8, 128), 0) + lax.broadcasted_iota(jnp.int32, (8, 128), 1)
    live = count[0, 0]
    keys = []
    for i in range(16):
        at = pl.ds(8 * i, 8)
        weight = jnp.where(slot + 1024 * i < live, wide[at, :] * 64.0, 0.0).astype(jnp.int32)
        row = zc[at, :] * PLANE + xc[at, :] + (XO - RIM - 4096)
        keys.append((row << 19) | (yc[at, :] << 12) | weight)
    keys = bitonic(keys)
    for i in range(16):
        raw[8 * i : 8 * i + 8, :] = keys[i]
    first = pltpu.make_async_copy(raw.at[pl.ds(0, 8)], ends.at[0], sem.at[0])
    last = pltpu.make_async_copy(raw.at[pl.ds(120, 8)], ends.at[1], sem.at[1])
    first.start()
    last.start()
    tidy[...] = raw[...].T
    zeros = jnp.zeros((PLANE, 128), F32)

    @pl.loop(0, CZ)
    def _(z):
        acc[pl.ds(pl.multiple_of(z * PLANE, 8), PLANE), :] = zeros

    first.wait()
    last.wait()
    ys = lax.broadcasted_iota(jnp.int32, (128, 128), 0)
    ws = lax.broadcasted_iota(jnp.int32, (WIN, 128), 0)

    def window(row, start, y_hot):
        hot = jnp.where(ws == row - start, 1.0, 0.0).astype(BF16)
        return lax.dot_general(hot, y_hot, (((1,), (1,)), ((), ())), preferred_element_type=F32)

    def block(b):
        key = tidy[pl.ds(b, 1), :]
        weight = (key & 4095).astype(F32) * (1.0 / 64.0)
        y_hot = jnp.where(ys == ((key >> 12) & 127), weight, 0.0).astype(BF16)
        return (key >> 19) + 4096, y_hot

    def bounds(b):
        lo = (ends[0, 0, b] >> 19) + 4096
        hi = (ends[1, 7, b] >> 19) + 4096
        start = jnp.minimum((lo >> 3) << 3, ROWS - WIN)
        return pl.multiple_of(start, 8), (hi - start) >> 6

    @pl.loop(0, NBLK // UNROLL)
    def _(g):
        extra = 0
        parts = []
        for u in range(UNROLL):
            b = g * UNROLL + u
            start, more = bounds(b)
            row, y_hot = block(b)
            parts.append((start, window(row, start, y_hot)))
            extra = extra + more
        for start, part in parts:
            acc[pl.ds(start, WIN), :] += part

        @pl.when(extra > 0)
        def _():
            for u in range(UNROLL):
                b = g * UNROLL + u
                start, more = bounds(b)

                @pl.loop(0, more)
                def _(n):
                    begin = start + (n + 1) * WIN
                    place = pl.multiple_of(jnp.minimum(begin, ROWS - WIN), 8)
                    row, y_hot = block(b)
                    row = jnp.where(row >= begin, row, -1)
                    acc[pl.ds(place, WIN), :] += window(row, place, y_hot)

    @pl.loop(0, CZ)
    def _(z):
        plane = acc[pl.ds(pl.multiple_of(z * PLANE, 8), PLANE), :]
        out[z] = apply(plane, both[...], low[...])


def deposit(count, zc, xc, yc, mass, both, low):
    smem = pl.BlockSpec(memory_space=pltpu.SMEM)
    vmem = pl.BlockSpec(memory_space=pltpu.VMEM)
    return pl.pallas_call(
        deposit_kernel,
        out_shape=jax.ShapeDtypeStruct((CZ, PLANE, CY), F32),
        in_specs=[smem] + [vmem] * 6,
        out_specs=vmem,
        scratch_shapes=[
            pltpu.VMEM((ROWS, CY), F32),
            pltpu.VMEM((128, 128), F32),
            pltpu.VMEM((128, 128), jnp.int32),
            pltpu.VMEM((128, 128), jnp.int32),
            pltpu.SMEM((2, 8, 128), jnp.int32),
            pltpu.SemaphoreType.DMA((2,)),
        ],
        name="deposit",
    )(count, zc, xc, yc, mass, both, low)


def sweep(src, dst, lo, hi, center, d0, d1, z_live, x_live):
    @pl.loop(lo, hi)
    def _(z):
        live = z_live(z)
        c, a, b = center * live, d0 * live, d1 * live
        for n in range(34):
            r = 8 + 8 * n
            along_z = src[z - 1, r : r + 8, :] + src[z + 1, r : r + 8, :]
            along_x = src[z, r - 1 : r + 7, :] + src[z, r + 1 : r + 9, :]
            new = src[z, r : r + 8, :] * c + along_z * a + along_x * b
            if n == 0:
                new = new * x_live[0]
            if n == 33:
                new = new * x_live[1]
            dst[z, r : r + 8, :] = new


def back_to_cells(src, dst, grad, both, low):
    @pl.loop(HALO - 1, HALO + CZ + 1)
    def _(z):
        mixed = apply(src[z, 8:280, :], both[...], low[...])
        dst[z, 8:280, :] = mixed[:, :CY]
        grad[z - HALO + 1] = mixed[8:264, CY:]


def gradient(src, grad):
    @pl.loop(0, CZ)
    def _(z):
        for n in range(32):
            r = XO + 8 * n
            gz = src[z + HALO + 1, r : r + 8, :] - src[z + HALO - 1, r : r + 8, :]
            gx = src[z + HALO, r + 1 : r + 9, :] - src[z + HALO, r - 1 : r + 7, :]
            gy = grad[z + 1, 8 * n : 8 * n + 8, :]
            grad[z + 1, 8 * n : 8 * n + 8, :] = (gz * gz + gx * gx) * 0.25 + gy * gy


def render(dens, grad, out, slope, shift, scale):
    @pl.loop(0, CX // 32)
    def _(n):
        r = pl.multiple_of(32 * n, 32)
        keep = jnp.ones((32, CY), F32)
        for z in range(CZ):
            d = dens[z + HALO, pl.ds(r + XO, 32), :]
            g = grad[z + 1, pl.ds(r, 32), :]
            t = jnp.tanh(d * slope + shift)
            w = keep * (t * scale + scale)
            keep = keep - w
            sum_d = w * d if z == 0 else sum_d + w * d
            sum_g = w * g if z == 0 else sum_g + w * g
        out[0, pl.ds(r, 32), :] = sum_d
        out[1, pl.ds(r, 32), :] = sum_g
        out[2, pl.ds(r, 32), :] = keep


def image_kernel(
    dif, tfc, tfs, tfo, cosine, both, low, ext, out,
    one, two, left, right, grad, mine, came, whole, local_sem, halo_send, halo_recv, pair_send, pair_recv, far_send, far_recv,
):
    depth, cols = lax.axis_index("depth"), lax.axis_index("cols")
    nd, nc = lax.axis_size("depth"), lax.axis_size("cols")
    core, chip = depth % 2, depth // 2
    chips = nd // 2
    partner = (depth + 1 - 2 * core, cols)

    def beside(dz, dx):
        return ((depth + dz + nd) % nd, (cols + dx + nc) % nc)

    around = [(dz, dx) for dz in (-1, 0, 1) for dx in (-1, 0, 1) if dz or dx]
    barrier = pltpu.get_barrier_semaphore()
    friends = [beside(dz, dx) for dz, dx in around] + [((depth + 2 * n) % nd, cols) for n in (1, 2, 3)]
    for friend in friends:
        pl.semaphore_signal(barrier, inc=1, device_id=friend, device_id_type=MESH)
    inner = pltpu.make_async_copy(ext, one.at[pl.ds(HALO, CZ)], local_sem)
    inner.start()
    zeros = jnp.zeros((8, CY), F32)

    @pl.loop(0, DEEP)
    def _(z):
        two[z, 0:8, :] = zeros
        two[z, 280:288, :] = zeros

    for z in (*range(HALO), *range(HALO + CZ, DEEP)):
        one[z, 0:8, :] = zeros
        one[z, 280:288, :] = zeros
    pl.semaphore_wait(barrier, len(friends))

    planes = {1: (CZ - HALO, 0, HALO), 0: (0, HALO, CZ), -1: (0, HALO + CZ, HALO)}
    copies = []
    for n, (dz, dx) in enumerate(around):
        src, dst, count = planes[dz]
        if dx == 0:
            source = ext.at[pl.ds(src, count), pl.ds(8, 272)]
            target = one.at[pl.ds(dst, count), pl.ds(8, 272)]
        elif dx == 1:
            source, target = ext.at[pl.ds(src, count), pl.ds(264, 16)], left.at[pl.ds(dst, count)]
        else:
            source, target = ext.at[pl.ds(src, count), pl.ds(8, 16)], right.at[pl.ds(dst, count)]
        copies.append(
            pltpu.make_async_remote_copy(
                src_ref=source, dst_ref=target, send_sem=halo_send.at[n], recv_sem=halo_recv.at[n],
                device_id=beside(dz, dx), device_id_type=MESH,
            )
        )
    for copy in copies:
        copy.start()
    inner.wait()
    for copy in copies:
        copy.wait()

    has_left = jnp.where(cols > 0, 1.0, 0.0)
    has_right = jnp.where(cols < nc - 1, 1.0, 0.0)
    has_low = jnp.where(depth > 0, 1.0, 0.0)
    has_high = jnp.where(depth < nd - 1, 1.0, 0.0)

    def z_live(z):
        return jnp.where(z < HALO, has_low, jnp.where(z >= HALO + CZ, has_high, 1.0))

    @pl.loop(0, DEEP)
    def _(z):
        one[z, 8:16, :] = (one[z, 8:16, :] + left[z, 0:8, :]) * has_left
        one[z, 16:24, :] = one[z, 16:24, :] + left[z, 8:16, :] * has_left
        one[z, 264:272, :] = one[z, 264:272, :] + right[z, 0:8, :] * has_right
        one[z, 272:280, :] = (one[z, 272:280, :] + right[z, 8:16, :]) * has_right

    @pl.when(depth == 0)
    def _():
        for z in range(HALO):
            one[z] = jnp.zeros((PLANE, CY), F32)

    @pl.when(depth == nd - 1)
    def _():
        for z in range(HALO + CZ, DEEP):
            one[z] = jnp.zeros((PLANE, CY), F32)

    d0, d1, d2 = dif[0], dif[1], dif[2]
    center = cosine[...] * d2 + (1.0 - 2.0 * (d0 + d1 + d2))
    src, dst = one, two
    for s in range(SMOOTH):
        sweep(src, dst, s + 1, DEEP - s - 1, center, d0, d1, z_live, (has_left, has_right))
        src, dst = dst, src
    back_to_cells(src, dst, grad, both, low)
    gradient(dst, grad)

    def draw(k, target):
        sharp = 0.5 * tfs[k]
        render(dst, grad, target, sharp, -sharp * tfc[k], 0.5 * tfo[k])

    swaps = []
    for j in range(chips):
        i = (chip + (2, 1, 3, 0)[j]) % chips
        draw(2 * i + 1 - core, mine.at[j])
        swap = pltpu.make_async_remote_copy(
            src_ref=mine.at[j], dst_ref=came.at[j], send_sem=pair_send.at[j], recv_sem=pair_recv.at[j],
            device_id=partner, device_id_type=MESH,
        )
        swap.start()
        swaps.append(swap)
    sends = []
    for j in range(chips):
        i = (chip + (2, 1, 3, 0)[j]) % chips
        held = mine.at[chips + j]
        draw(2 * i + core, held)
        swaps[j].wait_recv()
        place = held if j < chips - 1 else whole.at[chip]

        @pl.loop(0, CX // 32)
        def _(n):
            at = pl.ds(pl.multiple_of(32 * n, 32), 32)
            first = [jnp.where(core == 0, held[q, at, :], came[j, q, at, :]) for q in range(3)]
            then = [jnp.where(core == 0, came[j, q, at, :], held[q, at, :]) for q in range(3)]
            place[0, at, :] = first[0] + first[2] * then[0]
            place[1, at, :] = first[1] + first[2] * then[1]
            place[2, at, :] = first[2] * then[2]

        if j < chips - 1:
            send = pltpu.make_async_remote_copy(
                src_ref=held, dst_ref=whole.at[chip], send_sem=far_send.at[j], recv_sem=far_recv.at[j],
                device_id=(2 * i + core, cols), device_id_type=MESH,
            )
            send.start()
            sends.append(send)
    for send in sends:
        send.wait()
    for swap in swaps:
        swap.wait_send()

    @pl.loop(0, CX // 32)
    def _(n):
        at = pl.ds(pl.multiple_of(32 * n, 32), 32)
        sum_d, sum_g, keep = (whole[chips - 1, q, at, :] for q in range(3))
        for i in range(chips - 2, -1, -1):
            near = whole[i, 2, at, :]
            sum_d = whole[i, 0, at, :] + near * sum_d
            sum_g = whole[i, 1, at, :] + near * sum_g
            keep = near * keep
        out[0, at, :] = sum_d
        out[1, at, :] = sum_g
        out[2, at, :] = keep


def image(dif, tfc, tfs, tfo, cosine, both, low, ext):
    smem = pl.BlockSpec(memory_space=pltpu.SMEM)
    vmem = pl.BlockSpec(memory_space=pltpu.VMEM)
    return pl.pallas_call(
        image_kernel,
        out_shape=jax.ShapeDtypeStruct((3, CX, CY), F32),
        in_specs=[smem] * 4 + [vmem] * 3 + [pl.BlockSpec(memory_space=pl.ANY)],
        out_specs=vmem,
        scratch_shapes=[
            pltpu.VMEM((DEEP, PLANE, CY), F32),
            pltpu.VMEM((DEEP, PLANE, CY), F32),
            pltpu.VMEM((DEEP, 16, CY), F32),
            pltpu.VMEM((DEEP, 16, CY), F32),
            pltpu.VMEM((CZ + 2, CX, CY), F32),
            pltpu.VMEM((TFS, 3, CX, CY), F32),
            pltpu.VMEM((4, 3, CX, CY), F32),
            pltpu.VMEM((4, 3, CX, CY), F32),
            pltpu.SemaphoreType.DMA,
            pltpu.SemaphoreType.DMA((8,)),
            pltpu.SemaphoreType.DMA((8,)),
            pltpu.SemaphoreType.DMA((4,)),
            pltpu.SemaphoreType.DMA((4,)),
            pltpu.SemaphoreType.DMA((3,)),
            pltpu.SemaphoreType.DMA((3,)),
        ],
        compiler_params=pltpu.CompilerParams(collective_id=0, has_side_effects=True, vmem_limit_bytes=56 << 20),
        name="image",
    )(dif, tfc, tfs, tfo, cosine, both, low, ext)


def shards(depth_cell, column_cell, row_cell, mass, counts, diffusion, tf_center, tf_sharp, tf_opacity, tf_shade, tf_color):
    s_both, s_low, b_both, b_low, cosine = (jnp.asarray(table) for table in tables())
    cells = [cell.reshape(128, 128) for cell in (depth_cell, column_cell, row_cell)]
    extended = deposit(counts, *cells, mass, s_both, s_low)
    dens, grad, keep = image(diffusion, tf_center, tf_sharp, tf_opacity, cosine, b_both, b_low, extended)
    depth = lax.axis_index("depth")
    tint = lax.dynamic_slice_in_dim(tf_color, depth, 1)[0]
    shade = lax.dynamic_slice_in_dim(tf_shade, depth, 1)
    colors = tint[:, None, None] * dens + shade[:, None, None] * grad
    return jnp.concatenate([colors, keep[None]], axis=0)


def solution(mesh):
    brick = P("depth", "cols", None)
    placed = (brick,) * 4 + (P("depth", "cols"),) + (P(),) * 6
    return jax.shard_map(shards, mesh=mesh, in_specs=placed, out_specs=brick, check_vma=False)
```

time: 122 us -> 72.7 us (0.60)
  the two profiles are of different devices: /device:TPU:6 before, /device:TPU:1 now
where the time goes in v2:
time: 72.7 us; the launch traced here: 72.8 us
  Pallas kernels  68.6 us (94%)
  other arithmetic  2.64 us (4%)
  local copies, waits for them, and re-layouts  0.79 us (1%)
    pallas_call x1, Pallas kernels, image(): pl.pallas_call(image_kernel, out_shape=jax.ShapeDtypeStruct((3, CX, CY),...  54.2 us
    pallas_call x1, Pallas kernels, deposit(): pl.pallas_call(deposit_kernel, out_shape=jax.ShapeDtypeStruct((CZ, PLANE,...  14.4 us
    mul x1, other arithmetic, shards(): colors = tint[:, None, None] * dens + shade[:, None, None] * grad  1.7 us

profile of v2, /device:TPU:1, one launch (start us, length us, event | category | flops | bytes accessed | tf_op | source)
XLA Modules:
  0.0 72.8 jit_solution(11987323118023424831)
XLA Ops:
  0.0 0.0 copy-start
  0.7 0.0 copy-start.1
  0.7 14.4 %deposit.1.ext = f32[16,288,128]{2,1,0:T(8,128)} custom-call(s32[1,1]{1,0:T(1,128)S(6)} %copy.17.count, s32[128,128]{1,0:T(8,128)} %bitcast.8, s32[128,128]{1,0:T(8,128)} %bitcast.9, s32[128,128]{1,0:T(8,128)} %bitcast.10, bf16[1,1,16384]{2,1,0:T(2,128)(2,1)} %mass.1, bf16[256,128]{1,0:T(8,128)(2,1)} %constant.20.clone.both, bf16[128,128]{1,0:T(8,128)(2,1)} %constant.21.clone.low), custom_call_target="tpu_custom_call" | custom-call | tf_op jit(solution)/shard_map/deposit/pallas_call | solution.py:175
  15.1 54.2 %image.1 = f32[3,256,128]{2,1,0:T(8,128)} custom-call(f32[3]{0:T(128)} %dif.1, f32[8]{0:T(128)} %tfc.1, f32[8]{0:T(128)} %tfs.1, f32[8]{0:T(128)} %tfo.1, f32[8,128]{1,0:T(8,128)} %constant.24.clone.cosine, bf16[256,256]{1,0:T(8,128)(2,1)} %constant.22.clone.both, bf16[128,256]{1,0:T(8,128)(2,1)} %constant.23.clone.low, f32[16,288,128]{2,1,0:T(8,128)} %deposit.1.ext), custom_call_target="tpu_custom_call" | custom-call | tf_op jit(solution)/shard_map/image/pallas_call | solution.py:395
  69.3 0.0 copy-done.1
  69.3 0.6 dynamic_slice.7
  69.9 1.7 %slice_bitcast_fusion = (f32[256,128]{1,0:T(8,128)S(1)}, f32[1,256,128]{2,1,0:T(8,128)S(1)}, f32[256,128]{1,0:T(8,128)S(1)}) fusion(f32[3,256,128]{2,1,0:T(8,128)} %image.1, f32[]{:T(128)} %bitcast.4), kind=kLoop, calls=%fused_computation.3 | loop fusion | flops 32768 | bytes 786436 | tf_op jit(solution)/shard_map/mul | solution.py:430
  71.6 0.0 copy-done
  71.6 0.2 dynamic-slice_reduce_fusion
  71.8 0.1 multiply_add_fusion
  71.9 0.8 %pad_maximum_fusion = f32[4,256,128]{2,1,0:T(8,128)} fusion(f32[1,256,128]{2,1,0:T(8,128)S(1)} %get-tuple-element.6, f32[3,256,128]{2,1,0:T(8,128)S(1)} %multiply_add_fusion), kind=kLoop, calls=%fused_computation | loop fusion | flops 131072 | bytes 1048576 | tf_op jit(solution)/shard_map/concatenate | solution.py:431
Async XLA Ops:
  0.0 71.6 %copy-start = (f32[8,3]{0,1:T(4,128)S(1)}, f32[8,3]{0,1:T(4,128)}, u32[]{:S(2)}) copy-start(f32[8,3]{0,1:T(4,128)} %param.26) | copy-start | bytes 292
  0.7 68.6 %copy-start.1 = (f32[8]{0:T(128)S(1)}, f32[8]{0:T(128)}, u32[]{:S(2)}) copy-start(f32[8]{0:T(128)} %param.25) | copy-start | bytes 100

commit v3 on v2

v3 whole, which is shorter than its diff:
```python
import functools

import jax
import jax.numpy as jnp
import numpy as np
from jax import lax
from jax.experimental import pallas as pl
from jax.experimental.pallas import tpu as pltpu
from jax.sharding import PartitionSpec as P

CZ, CX, CY, RIM = 16, 256, 128, 4
SMOOTH, TFS = 4, 8
HALO = SMOOTH + 1
DEEP = CZ + 2 * HALO
PLANE = 288
XO = 16
ROWS = CZ * PLANE
WIN = 64
UNROLL = 16
SLOTS = 16384
NBLK = SLOTS // 128
MESH = pl.DeviceIdType.MESH
F32, BF16 = jnp.float32, jnp.bfloat16


def split(matrix):
    top = matrix.astype(BF16)
    return top, (matrix - top.astype(np.float64)).astype(BF16)


def tables():
    n = np.arange(1, CY + 1, dtype=np.float64)
    sine = np.sqrt(2.0 / (CY + 1)) * np.sin(np.pi * np.outer(n, n) / (CY + 1))
    slope = 0.5 * (np.eye(CY, k=-1) - np.eye(CY, k=1))
    s_top, s_low = split(sine)
    b_top, b_low = split(np.concatenate([sine, sine @ slope], axis=1))
    cosine = np.broadcast_to(2.0 * np.cos(np.pi * n / (CY + 1)), (8, CY)).astype(np.float32)
    forth = np.block([[s_top, s_low], [s_top, np.zeros_like(s_low)]])
    return forth, np.concatenate([b_top, b_top]), b_low, cosine


def pair_of(value):
    top = value.astype(BF16)
    return top, (value - top.astype(F32)).astype(BF16)


def exchange(x, stride, axis, bit):
    size = x.shape[axis]
    up = pltpu.roll(x, size - stride, axis)
    down = up if 2 * stride == size else pltpu.roll(x, stride, axis)
    return jnp.where(bit, jnp.maximum(x, down), jnp.minimum(x, up))


def bitonic(vs):
    lane = lax.broadcasted_iota(jnp.int32, (8, 128), 1)
    sub = lax.broadcasted_iota(jnp.int32, (8, 128), 0)
    bits = {j: (sub >> (j - 4)) & 1 if j < 7 else (lane >> (j - 7)) & 1 for j in range(4, 14)}
    hot = {j: bits[j] == 1 for j in bits}
    neg = {j: -bits[j] for j in bits}

    def flips(j, i):
        if j == 0 or j == 14:
            return 0
        return -((i >> j) & 1) if j < 4 else neg[j]

    for k in range(1, 15):
        out = []
        for i, v in enumerate(vs):
            a, b = flips(k - 1, i), flips(k, i)
            if isinstance(a, int) and isinstance(b, int):
                out.append(~v if a != b else v)
            else:
                out.append(v ^ (a ^ b))
        vs = out
        for j in range(k - 1, 6 if k == 14 else -1, -1):
            if j >= 7:
                vs = [exchange(v, 1 << (j - 7), 1, hot[j]) for v in vs]
            elif j >= 4:
                vs = [exchange(v, 1 << (j - 4), 0, hot[j]) for v in vs]
            else:
                out = list(vs)
                for i in range(16):
                    p = i ^ (1 << j)
                    if i < p:
                        out[i] = jnp.minimum(vs[i], vs[p])
                        out[p] = jnp.maximum(vs[i], vs[p])
                vs = out
    return vs


def deposit_kernel(count, zc, xc, yc, mass, forth, out, acc, wide, raw, tidy, range_of, ends, sem):
    for i in range(128):
        wide[i : i + 1, :] = mass[0, 0:1, 128 * i : 128 * i + 128].astype(F32)
    slot = 128 * lax.broadcasted_iota(jnp.int32, (8, 128), 0) + lax.broadcasted_iota(jnp.int32, (8, 128), 1)
    live = count[0, 0]
    keys = []
    for i in range(16):
        at = pl.ds(8 * i, 8)
        weight = jnp.where(slot + 1024 * i < live, wide[at, :] * 64.0, 0.0).astype(jnp.int32)
        row = zc[at, :] * PLANE + xc[at, :] + (XO - RIM - 4096)
        keys.append((row << 19) | (yc[at, :] << 12) | weight)
    keys = bitonic(keys)
    for i in range(16):
        raw[8 * i : 8 * i + 8, :] = keys[i]
    range_of[0] = jnp.broadcast_to(jnp.min(functools.reduce(jnp.minimum, keys), axis=0, keepdims=True), (8, 128))
    range_of[1] = jnp.broadcast_to(jnp.max(functools.reduce(jnp.maximum, keys), axis=0, keepdims=True), (8, 128))
    tidy[...] = raw[...].T
    zeros = jnp.zeros((PLANE, 128), F32)

    @pl.loop(0, CZ)
    def _(z):
        acc[pl.ds(pl.multiple_of(z * PLANE, 8), PLANE), :] = zeros

    found = pltpu.make_async_copy(range_of, ends, sem)
    found.start()
    found.wait()
    ys = lax.broadcasted_iota(jnp.int32, (128, 128), 0)
    ws = lax.broadcasted_iota(jnp.int32, (WIN, 128), 0)

    def window(row, start, y_hot):
        hot = jnp.where(ws == row - start, 1.0, 0.0).astype(BF16)
        return lax.dot_general(hot, y_hot, (((1,), (1,)), ((), ())), preferred_element_type=F32)

    def block(b):
        key = tidy[pl.ds(b, 1), :]
        weight = (key & 4095).astype(F32) * (1.0 / 64.0)
        y_hot = jnp.where(ys == ((key >> 12) & 127), weight, 0.0).astype(BF16)
        return (key >> 19) + 4096, y_hot

    def bounds(b):
        lo = (ends[0, 0, b] >> 19) + 4096
        hi = (ends[1, 0, b] >> 19) + 4096
        start = jnp.minimum((lo >> 3) << 3, ROWS - WIN)
        return pl.multiple_of(start, 8), (hi - start) >> 6

    @pl.loop(0, NBLK // UNROLL)
    def _(g):
        extra = 0
        parts = []
        for u in range(UNROLL):
            b = g * UNROLL + u
            start, more = bounds(b)
            row, y_hot = block(b)
            parts.append((start, window(row, start, y_hot)))
            extra = extra + more
        for start, part in parts:
            acc[pl.ds(start, WIN), :] += part

        @pl.when(extra > 0)
        def _():
            @pl.loop(0, UNROLL)
            def _(u):
                b = g * UNROLL + u
                start, more = bounds(b)

                @pl.loop(0, more)
                def _(n):
                    begin = start + (n + 1) * WIN
                    place = pl.multiple_of(jnp.minimum(begin, ROWS - WIN), 8)
                    row, y_hot = block(b)
                    row = jnp.where(row >= begin, row, -1)
                    acc[pl.ds(place, WIN), :] += window(row, place, y_hot)

    @pl.loop(0, CZ)
    def _(z):
        plane = acc[pl.ds(pl.multiple_of(z * PLANE, 8), PLANE), :]
        both = jnp.dot(jnp.concatenate(pair_of(plane), axis=1), forth[...], preferred_element_type=F32)
        out[z] = both[:, :CY] + both[:, CY:]


def deposit(count, zc, xc, yc, mass, forth):
    smem = pl.BlockSpec(memory_space=pltpu.SMEM)
    vmem = pl.BlockSpec(memory_space=pltpu.VMEM)
    return pl.pallas_call(
        deposit_kernel,
        out_shape=jax.ShapeDtypeStruct((CZ, PLANE, CY), F32),
        in_specs=[smem] + [vmem] * 5,
        out_specs=vmem,
        scratch_shapes=[
            pltpu.VMEM((ROWS, CY), F32),
            pltpu.VMEM((128, 128), F32),
            pltpu.VMEM((128, 128), jnp.int32),
            pltpu.VMEM((128, 128), jnp.int32),
            pltpu.VMEM((2, 8, 128), jnp.int32),
            pltpu.SMEM((2, 8, 128), jnp.int32),
            pltpu.SemaphoreType.DMA,
        ],
        compiler_params=pltpu.CompilerParams(vmem_limit_bytes=12 << 20),
        name="deposit",
    )(count, zc, xc, yc, mass, forth)


CHUNK = 64
CHUNKS = CX // CHUNK
SPAN = CHUNK + 16
ORDER = (1, 2, 0, 3)
PARTS = ((64, 96), (160, 64), (8, 56), (224, 56))


def sweep(src, at, dst, lo, hi, center, d0, d1, z_live, x_live):
    @pl.loop(lo, hi, step=2)
    def _(base):
        for z in (base, base + 1):
            live = z_live(z)
            c, a, b = center * live, d0 * live, d1 * live
            for n in range(SPAN // 8):
                r = at + 8 * n
                along_z = src[z - 1, r : r + 8, :] + src[z + 1, r : r + 8, :]
                along_x = src[z, r - 1 : r + 7, :] + src[z, r + 1 : r + 9, :]
                new = src[z, r : r + 8, :] * c + along_z * a + along_x * b
                if n in x_live:
                    new = new * x_live[n]
                dst[z, 8 + 8 * n : 16 + 8 * n, :] = new


def back_to_cells(src, dst, grad, back, back_low):
    @pl.loop(0, (CZ + 2) // 2)
    def _(step):
        for half in range(2):
            z = step * 2 + half
            top, rest = pair_of(src[z + HALO - 1, 8 : 8 + SPAN, :])
            mixed = jnp.dot(jnp.concatenate([top, rest], axis=1), back[...], preferred_element_type=F32)
            mixed = mixed + jnp.dot(top, back_low[...], preferred_element_type=F32)
            dst[z + HALO - 1, 8 : 8 + SPAN, :] = mixed[:, :CY]
            grad[z] = mixed[8 : 8 + CHUNK, CY:]


def gradient(src, grad):
    @pl.loop(0, CZ // 2)
    def _(step):
        for half in range(2):
            z = step * 2 + half
            for n in range(CHUNK // 8):
                r = 16 + 8 * n
                gz = src[z + HALO + 1, r : r + 8, :] - src[z + HALO - 1, r : r + 8, :]
                gx = src[z + HALO, r + 1 : r + 9, :] - src[z + HALO, r - 1 : r + 7, :]
                gy = grad[z + 1, 8 * n : 8 * n + 8, :]
                grad[z + 1, 8 * n : 8 * n + 8, :] = (gz * gz + gx * gx) * 0.25 + gy * gy


def render(dens, grad, out, r, slope, shift, scale):
    keep = jnp.ones((32, CY), F32)
    for z in range(CZ):
        d = dens[z + HALO, pl.ds(r + 16, 32), :]
        g = grad[z + 1, pl.ds(r, 32), :]
        t = jnp.tanh(d * slope + shift)
        w = keep * (t * scale + scale)
        keep = keep - w
        sum_d = w * d if z == 0 else sum_d + w * d
        sum_g = w * g if z == 0 else sum_g + w * g
    out[0, pl.ds(r, 32), :] = sum_d
    out[1, pl.ds(r, 32), :] = sum_g
    out[2, pl.ds(r, 32), :] = keep


def image_kernel(
    dif, tfc, tfs, tfo, shade, tint, cosine, back, back_low, ext, out,
    one, ta, tb, left, right, grad, mine, came, whole,
    local_sem, side_send, side_recv, halo_send, halo_recv, pair_send, pair_recv, far_send, far_recv,
):
    depth, cols = lax.axis_index("depth"), lax.axis_index("cols")
    nd, nc = lax.axis_size("depth"), lax.axis_size("cols")
    core, chip = depth % 2, depth // 2
    chips = nd // 2
    partner = (depth + 1 - 2 * core, cols)

    def beside(dz, dx):
        return ((depth + dz + nd) % nd, (cols + dx + nc) % nc)

    around = [(dz, dx) for dz in (-1, 0, 1) for dx in (-1, 0, 1) if dz or dx]
    barrier = pltpu.get_barrier_semaphore()
    friends = [beside(dz, dx) for dz, dx in around] + [((depth + 2 * n) % nd, cols) for n in (1, 2, 3)]
    for friend in friends:
        pl.semaphore_signal(barrier, inc=1, device_id=friend, device_id_type=MESH)
    inner = pltpu.make_async_copy(ext, one.at[pl.ds(HALO, CZ)], local_sem)
    inner.start()
    zeros = jnp.zeros((8, CY), F32)

    @pl.loop(0, DEEP)
    def _(z):
        for t in (ta, tb):
            t[z, 0:8, :] = zeros
            t[z, 8 + SPAN : 16 + SPAN, :] = zeros

    for z in (*range(HALO), *range(HALO + CZ, DEEP)):
        one[z, 0:8, :] = zeros
        one[z, 280:288, :] = zeros
    pl.semaphore_wait(barrier, len(friends))

    planes = {1: (CZ - HALO, 0, HALO), 0: (0, HALO, CZ), -1: (0, HALO + CZ, HALO)}

    def copy_to(source, target, send, recv, device):
        copy = pltpu.make_async_remote_copy(
            src_ref=source, dst_ref=target, send_sem=send, recv_sem=recv, device_id=device, device_id_type=MESH
        )
        copy.start()
        return copy

    halos, sides = {}, {-1: [], 1: []}

    def send_halo(step):
        begin, rows = PARTS[step]
        for n, dz in enumerate((-1, 1)):
            src, dst, count = planes[dz]
            halos[step, dz] = copy_to(
                ext.at[pl.ds(src, count), pl.ds(begin, rows)], one.at[pl.ds(dst, count), pl.ds(begin, rows)],
                halo_send.at[step, n], halo_recv.at[step, n], beside(dz, 0),
            )

    send_halo(0)
    for n, (dz, dx) in enumerate((dz, dx) for dx in (1, -1) for dz in (-1, 0, 1)):
        src, dst, count = planes[dz]
        sides[dx].append(
            copy_to(
                ext.at[pl.ds(src, count), pl.ds(264 if dx == 1 else 8, 16)],
                (left if dx == 1 else right).at[pl.ds(dst, count)],
                side_send.at[n], side_recv.at[n], beside(dz, dx),
            )
        )
    for step in range(1, CHUNKS):
        send_halo(step)
    inner.wait()

    has_left = jnp.where(cols > 0, 1.0, 0.0)
    has_right = jnp.where(cols < nc - 1, 1.0, 0.0)
    has_low = jnp.where(depth > 0, 1.0, 0.0)
    has_high = jnp.where(depth < nd - 1, 1.0, 0.0)

    def z_live(z):
        return jnp.where(z < HALO, has_low, jnp.where(z >= HALO + CZ, has_high, 1.0))

    d0, d1, d2 = dif[0], dif[1], dif[2]
    center = cosine[...] * d2 + (1.0 - 2.0 * (d0 + d1 + d2))

    def assemble(step):
        begin, rows = PARTS[step]
        halos[step, -1].wait()
        halos[step, 1].wait()

        @pl.when(depth == 0)
        def _():
            for z in range(HALO):
                one[z, begin : begin + rows, :] = jnp.zeros((rows, CY), F32)

        @pl.when(depth == nd - 1)
        def _():
            for z in range(HALO + CZ, DEEP):
                one[z, begin : begin + rows, :] = jnp.zeros((rows, CY), F32)

        if ORDER[step] == 0:
            for copy in sides[1]:
                copy.wait()

            @pl.loop(0, DEEP)
            def _(z):
                live = z_live(z) * has_left
                one[z, 8:16, :] = one[z, 8:16, :] * has_left + left[z, 0:8, :] * live
                one[z, 16:24, :] = one[z, 16:24, :] + left[z, 8:16, :] * live

        if ORDER[step] == CHUNKS - 1:
            for copy in sides[-1]:
                copy.wait()

            @pl.loop(0, DEEP)
            def _(z):
                live = z_live(z) * has_right
                one[z, 264:272, :] = one[z, 264:272, :] + right[z, 0:8, :] * live
                one[z, 272:280, :] = one[z, 272:280, :] * has_right + right[z, 8:16, :] * live

    def draw(chunk, own):
        @pl.loop(0, chips * (CHUNK // 32))
        def _(n):
            j = n // (CHUNK // 32)
            r = pl.multiple_of((n % (CHUNK // 32)) * 32, 32)
            k = 2 * ((chip + j + 2) % chips) + (core if own else 1 - core)
            sharp = 0.5 * tfs[k]
            render(ta, grad, mine.at[chunk, j + (chips if own else 0)], r, sharp, -sharp * tfc[k], 0.5 * tfo[k])

    swaps, sends = {}, []

    def combine(chunk):
        swaps[chunk].wait_recv()
        for j in range(chips):
            i = (chip + j + 2) % chips
            held = mine.at[chunk, chips + j]
            place = whole.at[chip, chunk] if j == 2 else held
            for n in range(CHUNK // 32):
                at = pl.ds(32 * n, 32)
                first = [jnp.where(core == 0, held[q, at, :], came[chunk, j, q, at, :]) for q in range(3)]
                then = [jnp.where(core == 0, came[chunk, j, q, at, :], held[q, at, :]) for q in range(3)]
                place[0, at, :] = first[0] + first[2] * then[0]
                place[1, at, :] = first[1] + first[2] * then[1]
                place[2, at, :] = first[2] * then[2]
            if j != 2:
                m = j - j // 3
                sends.append(
                    copy_to(
                        held, whole.at[chip, chunk], far_send.at[chunk, m], far_recv.at[chunk, m],
                        (2 * i + core, cols),
                    )
                )

    for step in range(CHUNKS):
        chunk = ORDER[step]
        assemble(step)
        x_live = {0: has_left} if chunk == 0 else {SPAN // 8 - 1: has_right} if chunk == CHUNKS - 1 else {}
        sweep(one, 8 + CHUNK * chunk, ta, 1, DEEP - 1, center, d0, d1, z_live, x_live)
        sweep(ta, 8, tb, 2, DEEP - 2, center, d0, d1, z_live, x_live)
        if step:
            combine(ORDER[step - 1])
        sweep(tb, 8, ta, 3, DEEP - 3, center, d0, d1, z_live, x_live)
        sweep(ta, 8, tb, 4, DEEP - 4, center, d0, d1, z_live, x_live)
        back_to_cells(tb, ta, grad, back, back_low)
        gradient(ta, grad)
        draw(chunk, False)
        swaps[chunk] = copy_to(
            mine.at[chunk, pl.ds(0, chips)], came.at[chunk], pair_send.at[chunk], pair_recv.at[chunk], partner
        )
        draw(chunk, True)
    combine(ORDER[-1])

    color = [tint[q, depth] for q in range(3)]
    shading = shade[depth]
    for step in range(CHUNKS):
        for send in sends[3 * step : 3 * step + 3]:
            send.wait()
        chunk = ORDER[step]
        for n in range(CHUNK // 32):
            at = pl.ds(32 * n, 32)
            to = pl.ds(CHUNK * chunk + 32 * n, 32)
            sum_d, sum_g, keep = (whole[chips - 1, chunk, q, at, :] for q in range(3))
            for i in range(chips - 2, -1, -1):
                near = whole[i, chunk, 2, at, :]
                sum_d = whole[i, chunk, 0, at, :] + near * sum_d
                sum_g = whole[i, chunk, 1, at, :] + near * sum_g
                keep = near * keep
            for q in range(3):
                out[q, to, :] = sum_d * color[q] + sum_g * shading
            out[3, to, :] = keep
    for chunk in ORDER:
        swaps[chunk].wait_send()


def image(dif, tfc, tfs, tfo, shade, tint, cosine, back, back_low, ext):
    smem = pl.BlockSpec(memory_space=pltpu.SMEM)
    vmem = pl.BlockSpec(memory_space=pltpu.VMEM)
    return pl.pallas_call(
        image_kernel,
        out_shape=jax.ShapeDtypeStruct((4, CX, CY), F32),
        in_specs=[smem] * 6 + [vmem] * 3 + [pl.BlockSpec(memory_space=pl.ANY)],
        out_specs=vmem,
        scratch_shapes=[
            pltpu.VMEM((DEEP, PLANE, CY), F32),
            pltpu.VMEM((DEEP, SPAN + 16, CY), F32),
            pltpu.VMEM((DEEP, SPAN + 16, CY), F32),
            pltpu.VMEM((DEEP, 16, CY), F32),
            pltpu.VMEM((DEEP, 16, CY), F32),
            pltpu.VMEM((CZ + 2, CHUNK, CY), F32),
            pltpu.VMEM((CHUNKS, TFS, 3, CHUNK, CY), F32),
            pltpu.VMEM((CHUNKS, 4, 3, CHUNK, CY), F32),
            pltpu.VMEM((4, CHUNKS, 3, CHUNK, CY), F32),
            pltpu.SemaphoreType.DMA,
            pltpu.SemaphoreType.DMA((6,)),
            pltpu.SemaphoreType.DMA((6,)),
            pltpu.SemaphoreType.DMA((CHUNKS, 2)),
            pltpu.SemaphoreType.DMA((CHUNKS, 2)),
            pltpu.SemaphoreType.DMA((CHUNKS,)),
            pltpu.SemaphoreType.DMA((CHUNKS,)),
            pltpu.SemaphoreType.DMA((CHUNKS, 3)),
            pltpu.SemaphoreType.DMA((CHUNKS, 3)),
        ],
        compiler_params=pltpu.CompilerParams(collective_id=0, has_side_effects=True, vmem_limit_bytes=32 << 20),
        name="image",
    )(dif, tfc, tfs, tfo, shade, tint, cosine, back, back_low, ext)


def shards(depth_cell, column_cell, row_cell, mass, counts, diffusion, tf_center, tf_sharp, tf_opacity, tf_shade, tf_color):
    forth, back, back_low, cosine = (jnp.asarray(table) for table in tables())
    cells = [cell.reshape(128, 128) for cell in (depth_cell, column_cell, row_cell)]
    extended = deposit(counts, *cells, mass, forth)
    return image(
        diffusion, tf_center, tf_sharp, tf_opacity, tf_shade, tf_color.T, cosine, back, back_low, extended
    )


def solution(mesh):
    brick = P("depth", "cols", None)
    placed = (brick,) * 4 + (P("depth", "cols"),) + (P(),) * 6
    return jax.shard_map(shards, mesh=mesh, in_specs=placed, out_specs=brick, check_vma=False)
```

time: 72.7 us -> 62.3 us (0.86)
  Pallas kernels: 68.6 us -> 56 us
  local copies, waits for them, and re-layouts: 0.79 us -> 5.09 us
  other arithmetic: 2.64 us -> 0 us
    pallas_call x1, Pallas kernels: 54.2 us -> 44.1 us  [image(): pl.pallas_call(image_kernel, out_shape=jax.ShapeDtypeStruct((4, CX, CY),...]
    unnamed x4 -> x29, local copies, waits for them, and re-layouts: 0.01 us -> 5.09 us
    pallas_call x1, Pallas kernels: 14.4 us -> 11.9 us  [deposit(): pl.pallas_call(deposit_kernel, out_shape=jax.ShapeDtypeStruct((CZ, PLANE,...]
    mul x1 -> x0, other arithmetic: 1.7 us -> none  [shards(): colors = tint[:, None, None] * dens + shade[:, None, None] * grad]
    concatenate x1 -> x0, other arithmetic: 0.83 us -> none  [shards(): return jnp.concatenate([colors, keep[None]], axis=0)]
    dynamic_slice x2 -> x0, local copies, waits for them, and re-layouts: 0.78 us -> none  [the longest x1 0.59 us: shards(): shade = lax.dynamic_slice_in_dim(tf_shade, depth, 1)]
where the time goes in v3:
time: 62.3 us; the launch traced here: 61.9 us
  Pallas kernels  56 us (90%)
  local copies, waits for them, and re-layouts  5.09 us (8%)
  between operations  0.85 us (1%)
    pallas_call x1, Pallas kernels, image(): pl.pallas_call(image_kernel, out_shape=jax.ShapeDtypeStruct((4, CX, CY),...  44.1 us
    pallas_call x1, Pallas kernels, deposit(): pl.pallas_call(deposit_kernel, out_shape=jax.ShapeDtypeStruct((CZ, PLANE,...  11.9 us
    unnamed x29, local copies, waits for them, and re-layouts  5.09 us

profile of v3, /device:TPU:1, one launch (start us, length us, event | category | flops | bytes accessed | tf_op | source)
XLA Modules:
  0.0 61.9 jit_solution(10790648036309021552)
XLA Ops:
  0.0 0.0 copy-start.7
  0.0 0.0 copy-start.8
  0.0 0.0 copy-start.13
  0.0 0.0 copy-start.12
  0.0 0.0 copy-start.11
  0.0 0.0 copy-start.10
  0.0 0.0 copy-start.9
  0.8 0.0 copy-start
  0.8 0.9 %copy-done = bf16[256,256]{1,0:T(8,128)(2,1)S(1)} copy-done((bf16[256,256]{1,0:T(8,128)(2,1)S(1)}, bf16[256,256]{1,0:T(8,128)(2,1)}, u32[]{:S(2)}) %copy-start) | copy-done | bytes 131096
  1.7 0.0 copy-start.2
  1.7 0.8 %copy-done.2 = s32[1,1,16384]{2,1,0:T(1,128)S(1)} copy-done((s32[1,1,16384]{2,1,0:T(1,128)S(1)}, s32[1,1,16384]{2,1,0:T(1,128)}, u32[]{:S(2)}) %copy-start.2) | copy-done | bytes 65560
  2.5 0.0 copy-start.3
  2.5 0.8 %copy-done.3 = s32[1,1,16384]{2,1,0:T(1,128)S(1)} copy-done((s32[1,1,16384]{2,1,0:T(1,128)S(1)}, s32[1,1,16384]{2,1,0:T(1,128)}, u32[]{:S(2)}) %copy-start.3) | copy-done | bytes 65560
  3.4 0.0 copy-start.4
  3.4 0.8 %copy-done.4 = s32[1,1,16384]{2,1,0:T(1,128)S(1)} copy-done((s32[1,1,16384]{2,1,0:T(1,128)S(1)}, s32[1,1,16384]{2,1,0:T(1,128)}, u32[]{:S(2)}) %copy-start.4) | copy-done | bytes 65560
  4.2 0.0 copy-start.5
  4.2 0.8 %copy-done.5 = bf16[1,1,16384]{2,1,0:T(2,128)(2,1)S(1)} copy-done((bf16[1,1,16384]{2,1,0:T(2,128)(2,1)S(1)}, bf16[1,1,16384]{2,1,0:T(2,128)(2,1)}, u32[]{:S(2)}) %copy-start.5) | copy-done | bytes 32792
  5.0 0.0 copy-start.1
  5.0 0.0 copy-start.6
  5.0 11.9 %deposit.1.ext = f32[16,288,128]{2,1,0:T(8,128)S(1)} custom-call(s32[1,1]{1,0:T(1,128)S(6)} %copy.17.count, s32[128,128]{1,0:T(8,128)S(1)} %bitcast.4, s32[128,128]{1,0:T(8,128)S(1)} %bitcast.5, s32[128,128]{1,0:T(8,128)S(1)} %bitcast.6, bf16[1,1,16384]{2,1,0:T(2,128)(2,1)S(1)} %copy-done.5, bf16[256,256]{1,0:T(8,128)(2,1)S(1)} %copy-done), custom_call_target="tpu_custom_call" | custom-call | tf_op jit(solution)/shard_map/deposit/pallas_call | solution.py:174
  16.9 0.0 copy-done.7
  16.9 0.0 copy-done.8
  16.9 0.0 copy-done.13
  16.9 0.0 copy-done.12
  16.9 0.0 copy-done.11
  17.0 0.0 copy-done.10
  17.0 0.0 copy-done.9
  17.0 0.0 copy-done.1
  17.0 0.0 copy-done.6
  17.0 44.1 %image.1 = f32[4,256,128]{2,1,0:T(8,128)S(1)} custom-call(f32[3]{0:T(128)S(1)} %copy-done.9, f32[8]{0:T(128)S(1)} %copy-done.10, f32[8]{0:T(128)S(1)} %copy-done.11, f32[8]{0:T(128)S(1)} %copy-done.12, f32[8]{0:T(128)S(1)} %copy-done.13, f32[3,8]{1,0:T(4,128)S(1)} %bitcast.7, f32[8,128]{1,0:T(8,128)S(1)} %copy-done.7, bf16[256,256]{1,0:T(8,128)(2,1)S(1)} %copy-done.1, ...), custom_call_target="tpu_custom_call" | custom-call | tf_op jit(solution)/shard_map/image/pallas_call | solution.py:447
  61.1 0.8 %copy.18 = f32[4,256,128]{2,1,0:T(8,128)} copy(f32[4,256,128]{2,1,0:T(8,128)S(1)} %image.1) | data formatting | bytes 1048576
Async XLA Ops:
  0.0 16.9 %copy-start.7 = (f32[8,128]{1,0:T(8,128)S(1)}, f32[8,128]{1,0:T(8,128)}, u32[]{:S(2)}) copy-start(f32[8,128]{1,0:T(8,128)} %constant.11.clone.cosine) | copy-start | bytes 12292
  0.0 16.9 %copy-start.8 = (f32[8,3]{0,1:T(4,128)S(1)}, f32[8,3]{0,1:T(4,128)}, u32[]{:S(2)}) copy-start(f32[8,3]{0,1:T(4,128)} %param.25) | copy-start | bytes 292
  0.0 16.9 %copy-start.13 = (f32[8]{0:T(128)S(1)}, f32[8]{0:T(128)}, u32[]{:S(2)}) copy-start(f32[8]{0:T(128)} %shade.1) | copy-start | bytes 100
  0.0 16.9 %copy-start.12 = (f32[8]{0:T(128)S(1)}, f32[8]{0:T(128)}, u32[]{:S(2)}) copy-start(f32[8]{0:T(128)} %tfo.1) | copy-start | bytes 100
  0.0 16.9 %copy-start.11 = (f32[8]{0:T(128)S(1)}, f32[8]{0:T(128)}, u32[]{:S(2)}) copy-start(f32[8]{0:T(128)} %tfs.1) | copy-start | bytes 100
  0.0 16.9 %copy-start.10 = (f32[8]{0:T(128)S(1)}, f32[8]{0:T(128)}, u32[]{:S(2)}) copy-start(f32[8]{0:T(128)} %tfc.1) | copy-start | bytes 100
  0.0 16.9 %copy-start.9 = (f32[3]{0:T(128)S(1)}, f32[3]{0:T(128)}, u32[]{:S(2)}) copy-start(f32[3]{0:T(128)} %dif.1) | copy-start | bytes 40
  0.8 0.9 %copy-start = (bf16[256,256]{1,0:T(8,128)(2,1)S(1)}, bf16[256,256]{1,0:T(8,128)(2,1)}, u32[]{:S(2)}) copy-start(bf16[256,256]{1,0:T(8,128)(2,1)} %constant.8.clone.forth) | copy-start | bytes 393220
  1.7 0.8 %copy-start.2 = (s32[1,1,16384]{2,1,0:T(1,128)S(1)}, s32[1,1,16384]{2,1,0:T(1,128)}, u32[]{:S(2)}) copy-start(s32[1,1,16384]{2,1,0:T(1,128)} %param.15) | copy-start | bytes 196612
  2.5 0.8 %copy-start.3 = (s32[1,1,16384]{2,1,0:T(1,128)S(1)}, s32[1,1,16384]{2,1,0:T(1,128)}, u32[]{:S(2)}) copy-start(s32[1,1,16384]{2,1,0:T(1,128)} %param.16) | copy-start | bytes 196612
  3.4 0.8 %copy-start.4 = (s32[1,1,16384]{2,1,0:T(1,128)S(1)}, s32[1,1,16384]{2,1,0:T(1,128)}, u32[]{:S(2)}) copy-start(s32[1,1,16384]{2,1,0:T(1,128)} %param.17) | copy-start | bytes 196612
  4.2 0.8 %copy-start.5 = (bf16[1,1,16384]{2,1,0:T(2,128)(2,1)S(1)}, bf16[1,1,16384]{2,1,0:T(2,128)(2,1)}, u32[]{:S(2)}) copy-start(bf16[1,1,16384]{2,1,0:T(2,128)(2,1)} %mass.1) | copy-start | bytes 98308
  5.0 11.9 %copy-start.1 = (bf16[256,256]{1,0:T(8,128)(2,1)S(1)}, bf16[256,256]{1,0:T(8,128)(2,1)}, u32[]{:S(2)}) copy-start(bf16[256,256]{1,0:T(8,128)(2,1)} %constant.9.clone.back) | copy-start | bytes 393220
  5.0 11.9 %copy-start.6 = (bf16[128,256]{1,0:T(8,128)(2,1)S(1)}, bf16[128,256]{1,0:T(8,128)(2,1)}, u32[]{:S(2)}) copy-start(bf16[128,256]{1,0:T(8,128)(2,1)} %constant.10.clone.back_low) | copy-start | bytes 196612

commit v4 on v3

v4 whole, which is shorter than its diff:
```python
import functools

import jax
import jax.numpy as jnp
import numpy as np
from jax import lax
from jax.experimental import pallas as pl
from jax.experimental.pallas import tpu as pltpu
from jax.sharding import PartitionSpec as P

CZ, CX, CY, RIM = 16, 256, 128, 4
SMOOTH, TFS = 4, 8
HALO = SMOOTH + 1
DEEP = CZ + 2 * HALO
PLANE = 288
XO = 16
ROWS = CZ * PLANE
WIN = 112
UNROLL = 8
SLOTS = 16384
NBLK = SLOTS // 256
MESH = pl.DeviceIdType.MESH
F32, BF16 = jnp.float32, jnp.bfloat16


def split(matrix):
    top = matrix.astype(BF16)
    return top, (matrix - top.astype(np.float64)).astype(BF16)


def tables():
    n = np.arange(1, CY + 1, dtype=np.float64)
    sine = np.sqrt(2.0 / (CY + 1)) * np.sin(np.pi * np.outer(n, n) / (CY + 1))
    slope = 0.5 * (np.eye(CY, k=-1) - np.eye(CY, k=1))
    s_top, s_low = split(sine)
    b_top, b_low = split(np.concatenate([sine, sine @ slope], axis=1))
    cosine = np.broadcast_to(2.0 * np.cos(np.pi * n / (CY + 1)), (8, CY)).astype(np.float32)
    forth = np.block([[s_top, s_low], [s_top, np.zeros_like(s_low)]])
    return forth, np.concatenate([b_top, b_top]), b_low, cosine


def pair_of(value):
    top = value.astype(BF16)
    return top, (value - top.astype(F32)).astype(BF16)


def exchange(x, stride, axis, bit):
    size = x.shape[axis]
    up = pltpu.roll(x, size - stride, axis)
    down = up if 2 * stride == size else pltpu.roll(x, stride, axis)
    return jnp.where(bit, jnp.maximum(x, down), jnp.minimum(x, up))


def bitonic(vs):
    lane = lax.broadcasted_iota(jnp.int32, (8, 128), 1)
    sub = lax.broadcasted_iota(jnp.int32, (8, 128), 0)
    bits = {j: (sub >> (j - 4)) & 1 if j < 7 else (lane >> (j - 7)) & 1 for j in range(4, 14)}
    hot = {j: bits[j] == 1 for j in bits}
    neg = {j: -bits[j] for j in bits}

    def flips(j, i):
        if j == 0 or j == 14:
            return 0
        return -((i >> j) & 1) if j < 4 else neg[j]

    for k in range(1, 15):
        out = []
        for i, v in enumerate(vs):
            a, b = flips(k - 1, i), flips(k, i)
            if isinstance(a, int) and isinstance(b, int):
                out.append(~v if a != b else v)
            else:
                out.append(v ^ (a ^ b))
        vs = out
        for j in range(k - 1, 6 if k == 14 else -1, -1):
            if j >= 7:
                vs = [exchange(v, 1 << (j - 7), 1, hot[j]) for v in vs]
            elif j >= 4:
                vs = [exchange(v, 1 << (j - 4), 0, hot[j]) for v in vs]
            else:
                out = list(vs)
                for i in range(16):
                    p = i ^ (1 << j)
                    if i < p:
                        out[i] = jnp.minimum(vs[i], vs[p])
                        out[p] = jnp.maximum(vs[i], vs[p])
                vs = out
    return vs


def deposit_kernel(count, zh, xh, yh, mh, fh, out, acc, zc, xc, yc, mass, forth, wide, raw, tidy, range_of, ends, sem):
    loads = [
        pltpu.make_async_copy(source, target, sem.at[n])
        for n, (source, target) in enumerate(((mh, mass), (zh, zc), (xh, xc), (yh, yc), (fh, forth)))
    ]
    for load in loads:
        load.start()
    zeros = jnp.zeros((PLANE, 128), F32)

    @pl.loop(0, CZ)
    def _(z):
        acc[pl.ds(pl.multiple_of(z * PLANE, 8), PLANE), :] = zeros

    loads[0].wait()
    for i in range(128):
        wide[i : i + 1, :] = mass[0, 0:1, 128 * i : 128 * i + 128].astype(F32)
    for load in loads[1:]:
        load.wait()
    slot = 128 * lax.broadcasted_iota(jnp.int32, (8, 128), 0) + lax.broadcasted_iota(jnp.int32, (8, 128), 1)
    live = count[0, 0]
    keys = []
    for i in range(16):
        at = pl.ds(8 * i, 8)
        weight = jnp.where(slot + 1024 * i < live, wide[at, :] * 64.0, 0.0).astype(jnp.int32)
        row = zc[at, :] * PLANE + xc[at, :] + (XO - RIM - 4096)
        keys.append((row << 19) | (yc[at, :] << 12) | weight)
    keys = bitonic(keys)
    range_of[0] = jnp.broadcast_to(jnp.min(functools.reduce(jnp.minimum, keys), axis=0, keepdims=True), (8, 128))
    range_of[1] = jnp.broadcast_to(jnp.max(functools.reduce(jnp.maximum, keys), axis=0, keepdims=True), (8, 128))
    found = pltpu.make_async_copy(range_of, ends, sem.at[5])
    found.start()
    for i in range(16):
        raw[8 * i : 8 * i + 8, :] = keys[i]
    tidy[...] = raw[...].T
    found.wait()
    ys = lax.broadcasted_iota(jnp.int32, (128, 128), 0)
    ws = lax.broadcasted_iota(jnp.int32, (WIN, 128), 0)

    def block(b, start, begin):
        hots, y_hots = [], []
        for half in range(2):
            key = tidy[pl.ds(2 * b + half, 1), :]
            row = (key >> 19) + 4096
            if begin is not None:
                row = jnp.where(row >= begin, row, -1)
            hots.append(jnp.where(ws == row - start, 1.0, 0.0).astype(BF16))
            weight = (key & 4095).astype(F32) * (1.0 / 64.0)
            y_hots.append(jnp.where(ys == ((key >> 12) & 127), weight, 0.0).astype(BF16))
        hot, y_hot = jnp.concatenate(hots, axis=1), jnp.concatenate(y_hots, axis=1)
        return lax.dot_general(hot, y_hot, (((1,), (1,)), ((), ())), preferred_element_type=F32)

    def bounds(b):
        lo = (ends[0, 0, 2 * b] >> 19) + 4096
        hi = (ends[1, 0, 2 * b + 1] >> 19) + 4096
        start = jnp.minimum((lo >> 3) << 3, ROWS - WIN)
        return pl.multiple_of(start, 8), (hi - start) // WIN

    @pl.loop(0, NBLK // UNROLL)
    def _(g):
        extra = 0
        parts = []
        for u in range(UNROLL):
            b = g * UNROLL + u
            start, more = bounds(b)
            parts.append((start, block(b, start, None)))
            extra = extra + more
        for start, part in parts:
            acc[pl.ds(start, WIN), :] += part

        @pl.when(extra > 0)
        def _():
            @pl.loop(0, UNROLL)
            def _(u):
                b = g * UNROLL + u
                start, more = bounds(b)

                @pl.loop(0, more)
                def _(n):
                    begin = start + (n + 1) * WIN
                    place = pl.multiple_of(jnp.minimum(begin, ROWS - WIN), 8)
                    acc[pl.ds(place, WIN), :] += block(b, place, begin)

    @pl.loop(0, CZ // 4)
    def _(step):
        rows = acc[pl.ds(pl.multiple_of(step * (4 * PLANE), 8), 4 * PLANE), :]
        both = jnp.dot(jnp.concatenate(pair_of(rows), axis=1), forth[...], preferred_element_type=F32)
        out[pl.ds(step * 4, 4)] = (both[:, :CY] + both[:, CY:]).reshape(4, PLANE, CY)


def deposit(count, zc, xc, yc, mass, forth):
    hbm = pl.BlockSpec(memory_space=pltpu.HBM)
    return pl.pallas_call(
        deposit_kernel,
        out_shape=jax.ShapeDtypeStruct((CZ, PLANE, CY), F32),
        in_specs=[pl.BlockSpec(memory_space=pltpu.SMEM)] + [hbm] * 5,
        out_specs=pl.BlockSpec(memory_space=pltpu.VMEM),
        scratch_shapes=[
            pltpu.VMEM((ROWS, CY), F32),
            pltpu.VMEM((128, 128), jnp.int32),
            pltpu.VMEM((128, 128), jnp.int32),
            pltpu.VMEM((128, 128), jnp.int32),
            pltpu.VMEM((1, 1, SLOTS), BF16),
            pltpu.VMEM((2 * CY, 2 * CY), BF16),
            pltpu.VMEM((128, 128), F32),
            pltpu.VMEM((128, 128), jnp.int32),
            pltpu.VMEM((128, 128), jnp.int32),
            pltpu.VMEM((2, 8, 128), jnp.int32),
            pltpu.SMEM((2, 8, 128), jnp.int32),
            pltpu.SemaphoreType.DMA((6,)),
        ],
        compiler_params=pltpu.CompilerParams(vmem_limit_bytes=12 << 20),
        name="deposit",
    )(count, zc, xc, yc, mass, forth)


CHUNK = 64
CHUNKS = CX // CHUNK
SPAN = CHUNK + 16
ORDER = (1, 2, 0, 3)
PARTS = ((64, 96), (160, 64), (8, 56), (224, 56))


def sweep(src, at, dst, lo, hi, unroll, center, ratio, x_live):
    @pl.loop(0, (hi - lo) // unroll)
    def _(step):
        for n in range(SPAN // 8):
            r = at + 8 * n
            for u in range(unroll):
                z = lo + step * unroll + u
                along_z = src[z - 1, r : r + 8, :] + src[z + 1, r : r + 8, :]
                along_x = src[z, r - 1 : r + 7, :] + src[z, r + 1 : r + 9, :]
                new = src[z, r : r + 8, :] * center + along_x * ratio + along_z
                if n in x_live:
                    new = new * x_live[n]
                dst[z, 8 + 8 * n : 16 + 8 * n, :] = new


def back_to_cells(src, dst, grad, back, back_low, scale):
    rows = 6 * SPAN

    @pl.loop(0, (CZ + 2) // 6)
    def _(step):
        z = step * 6
        top, rest = pair_of(src[pl.ds(z + HALO - 1, 6), 8 : 8 + SPAN, :].reshape(rows, CY) * scale)
        mixed = jnp.dot(jnp.concatenate([top, rest], axis=1), back[...], preferred_element_type=F32)
        mixed = (mixed + jnp.dot(top, back_low[...], preferred_element_type=F32)).reshape(6, SPAN, 2 * CY)
        dst[pl.ds(z + HALO - 1, 6), 8 : 8 + SPAN, :] = mixed[:, :, :CY]
        grad[pl.ds(z, 6)] = mixed[:, 8 : 8 + CHUNK, CY:]


def gradient(src, grad, rise_d, rise_g):
    for n in range(CHUNK // 8):
        r, at = 16 + 8 * n, slice(8 * n, 8 * n + 8)
        for z in range(CZ):
            here = src[z + HALO, r : r + 8, :]
            before = src[z + HALO - 1, r : r + 8, :]
            gz = src[z + HALO + 1, r : r + 8, :] - before
            gx = src[z + HALO, r + 1 : r + 9, :] - src[z + HALO, r - 1 : r + 7, :]
            gy = grad[z + 1, at, :]
            square = (gz * gz + gx * gx) * 0.25 + gy * gy
            if z == 0:
                rise_g[0, at, :] = square
            else:
                rise_g[z, at, :] = square - last
                rise_d[z, at, :] = here - before
            last = square
        rise_g[CZ, at, :] = last


def render(dens, rise_d, rise_g, out, slope, shift, scale):
    rows = slice(16, 16 + CHUNK)
    over = 1.0 - scale
    sum_d, sum_g = dens[HALO, rows, :], rise_g[0]
    for z in range(CZ):
        t = jnp.tanh(dens[z + HALO, rows, :] * slope + shift)
        through = over - t * scale
        if z == 0:
            keep = through
        else:
            sum_d = sum_d + keep * rise_d[z]
            sum_g = sum_g + keep * rise_g[z]
            keep = keep * through
    out[0] = sum_d - keep * dens[HALO + CZ - 1, rows, :]
    out[1] = sum_g - keep * rise_g[CZ]
    out[2] = keep


def image_kernel(
    dif_h, tfc_h, tfs_h, tfo_h, shade_h, tint_h, cosine_h, back_h, low_h, ext, out,
    one, ta, tb, left, right, grad, rise_d, rise_g, mine, came, whole,
    dif, tfc, tfs, tfo, shade, tint, cosine, back, back_low,
    load_sem, local_sem, side_send, side_recv, halo_send, halo_recv, pair_send, pair_recv, far_send, far_recv,
):
    depth, cols = lax.axis_index("depth"), lax.axis_index("cols")
    nd, nc = lax.axis_size("depth"), lax.axis_size("cols")
    core, chip = depth % 2, depth // 2
    chips = nd // 2
    partner = (depth + 1 - 2 * core, cols)

    def beside(dz, dx):
        return ((depth + dz + nd) % nd, (cols + dx + nc) % nc)

    barrier = pltpu.get_barrier_semaphore()
    friends = [beside(-1, 0), beside(1, 0), beside(0, -1), beside(0, 1)]
    friends += [((depth + 2 * n) % nd, cols) for n in range(1, chips)]
    for friend in friends:
        pl.semaphore_signal(barrier, inc=1, device_id=friend, device_id_type=MESH)
    pairs = (
        (dif_h, dif), (tfc_h, tfc), (tfs_h, tfs), (tfo_h, tfo), (shade_h, shade), (tint_h, tint),
        (cosine_h, cosine), (back_h, back), (low_h, back_low),
    )
    loads = [pltpu.make_async_copy(source, target, load_sem.at[n]) for n, (source, target) in enumerate(pairs)]
    inner = pltpu.make_async_copy(ext, one.at[pl.ds(HALO, CZ)], local_sem)
    inner.start()
    for load in loads:
        load.start()
    zeros = jnp.zeros((8, CY), F32)

    @pl.loop(0, DEEP)
    def _(z):
        for t in (ta, tb):
            t[z, 0:8, :] = zeros
            t[z, 8 + SPAN : 16 + SPAN, :] = zeros

    for z in (*range(HALO), *range(HALO + CZ, DEEP)):
        one[z, 0:8, :] = zeros
        one[z, 280:288, :] = zeros
    pl.semaphore_wait(barrier, len(friends))

    planes = {1: (CZ - HALO, 0, HALO), -1: (0, HALO + CZ, HALO)}

    def copy_to(source, target, send, recv, device):
        copy = pltpu.make_async_remote_copy(
            src_ref=source, dst_ref=target, send_sem=send, recv_sem=recv, device_id=device, device_id_type=MESH
        )
        copy.start()
        return copy

    halos, sides = [], []

    def send_side(n, source, begin, count, at):
        for m, dx, target in ((0, 1, left), (1, -1, right)):
            sides.append(
                copy_to(
                    source.at[pl.ds(begin, count), pl.ds(264 if dx == 1 else 8, 16)], target.at[pl.ds(at, count)],
                    side_send.at[n, m], side_recv.at[n, m], beside(0, dx),
                )
            )

    for step, (begin, rows) in enumerate(PARTS):
        for n, dz in enumerate((-1, 1)):
            src, dst, count = planes[dz]
            halos.append(
                copy_to(
                    ext.at[pl.ds(src, count), pl.ds(begin, rows)], one.at[pl.ds(dst, count), pl.ds(begin, rows)],
                    halo_send.at[step, n], halo_recv.at[step, n], beside(dz, 0),
                )
            )
    send_side(0, ext, 0, CZ, HALO)
    inner.wait()
    for load in loads:
        load.wait()

    has_left = jnp.where(cols > 0, 1.0, 0.0)
    has_right = jnp.where(cols < nc - 1, 1.0, 0.0)
    d0, d1, d2 = dif[0], dif[1], dif[2]
    along = jnp.full((8, CY), d0, F32)
    center = (cosine[...] * d2 + (1.0 - 2.0 * (d0 + d1 + d2))) / along
    ratio = jnp.full((8, CY), d1, F32) / along
    square = d0 * d0

    def clear(ref, first, begin, rows):
        @pl.when(depth == 0)
        def _():
            for z in range(first, HALO):
                ref[z, begin : begin + rows, :] = jnp.zeros((rows, CY), F32)

        @pl.when(depth == nd - 1)
        def _():
            for z in range(HALO + CZ, DEEP - first):
                ref[z, begin : begin + rows, :] = jnp.zeros((rows, CY), F32)

    def arrive(step):
        for halo in halos[2 * step : 2 * step + 2]:
            halo.wait()

    def draw(chunk, own):
        @pl.loop(0, chips)
        def _(j):
            k = 2 * ((chip + j + 2) % chips) + (core if own else 1 - core)
            sharp = 0.5 * tfs[k]
            out_ref = mine.at[chunk, j + (chips if own else 0)]
            render(ta, rise_d, rise_g, out_ref, sharp, -sharp * tfc[k], 0.5 * tfo[k])

    swaps, sends = {}, []

    def combine(chunk):
        swaps[chunk].wait_recv()
        for j in range(chips):
            i = (chip + j + 2) % chips
            held = mine.at[chunk, chips + j]
            place = whole.at[chip, chunk] if j == 2 else held
            for n in range(CHUNK // 32):
                at = pl.ds(32 * n, 32)
                first = [jnp.where(core == 0, held[q, at, :], came[chunk, j, q, at, :]) for q in range(3)]
                then = [jnp.where(core == 0, came[chunk, j, q, at, :], held[q, at, :]) for q in range(3)]
                place[0, at, :] = first[0] + first[2] * then[0]
                place[1, at, :] = first[1] + first[2] * then[1]
                place[2, at, :] = first[2] * then[2]
            if j != 2:
                m = j - j // 3
                sends.append(
                    copy_to(
                        held, whole.at[chip, chunk], far_send.at[chunk, m], far_recv.at[chunk, m],
                        (2 * i + core, cols),
                    )
                )

    for step in range(CHUNKS):
        chunk = ORDER[step]
        if step < 2:
            arrive(step)
            clear(one, 0, *PARTS[step])
        if step == 2:
            for side in sides:
                side.wait()

            @pl.loop(0, DEEP)
            def _(z):
                one[z, 8:16, :] = (one[z, 8:16, :] + left[z, 0:8, :]) * has_left
                one[z, 16:24, :] = one[z, 16:24, :] + left[z, 8:16, :] * has_left
                one[z, 264:272, :] = one[z, 264:272, :] + right[z, 0:8, :] * has_right
                one[z, 272:280, :] = (one[z, 272:280, :] + right[z, 8:16, :]) * has_right

            clear(one, 0, *PARTS[2])
            clear(one, 0, *PARTS[3])
        x_live = {0: has_left} if chunk == 0 else {SPAN // 8 - 1: has_right} if chunk == CHUNKS - 1 else {}
        sweep(one, 8 + CHUNK * chunk, ta, 1, DEEP - 1, 8, center, ratio, x_live)
        clear(ta, 1, 8, SPAN)
        sweep(ta, 8, tb, 2, DEEP - 2, 11, center, ratio, x_live)
        clear(tb, 2, 8, SPAN)
        if step:
            combine(ORDER[step - 1])
        sweep(tb, 8, ta, 3, DEEP - 3, 10, center, ratio, x_live)
        clear(ta, 3, 8, SPAN)
        sweep(ta, 8, tb, 4, DEEP - 4, 9, center, ratio, x_live)
        clear(tb, 4, 8, SPAN)
        if step == 1:
            arrive(2)
            arrive(3)
            send_side(1, one, 0, HALO, 0)
            send_side(2, one, HALO + CZ, HALO, HALO + CZ)
        back_to_cells(tb, ta, grad, back, back_low, square * square)
        gradient(ta, grad, rise_d, rise_g)
        draw(chunk, False)
        swaps[chunk] = copy_to(
            mine.at[chunk, pl.ds(0, chips)], came.at[chunk], pair_send.at[chunk], pair_recv.at[chunk], partner
        )
        draw(chunk, True)
    combine(ORDER[-1])

    color = [tint[q, depth] for q in range(3)]
    shading = shade[depth]
    for step in range(CHUNKS):
        for send in sends[3 * step : 3 * step + 3]:
            send.wait()
        chunk = ORDER[step]
        for n in range(CHUNK // 32):
            at = pl.ds(32 * n, 32)
            to = pl.ds(CHUNK * chunk + 32 * n, 32)
            sum_d, sum_g, keep = (whole[chips - 1, chunk, q, at, :] for q in range(3))
            for i in range(chips - 2, -1, -1):
                near = whole[i, chunk, 2, at, :]
                sum_d = whole[i, chunk, 0, at, :] + near * sum_d
                sum_g = whole[i, chunk, 1, at, :] + near * sum_g
                keep = near * keep
            for q in range(3):
                out[q, to, :] = sum_d * color[q] + sum_g * shading
            out[3, to, :] = keep
    for chunk in ORDER:
        swaps[chunk].wait_send()


def image(*operands):
    tall = pltpu.VMEM((DEEP, SPAN + 16, CY), F32)
    strip = pltpu.VMEM((DEEP, 16, CY), F32)
    return pl.pallas_call(
        image_kernel,
        out_shape=jax.ShapeDtypeStruct((4, CX, CY), F32),
        in_specs=[pl.BlockSpec(memory_space=pl.ANY)] * 10,
        out_specs=pl.BlockSpec(memory_space=pltpu.VMEM),
        scratch_shapes=[
            pltpu.VMEM((DEEP, PLANE, CY), F32),
            tall,
            tall,
            strip,
            strip,
            pltpu.VMEM((CZ + 2, CHUNK, CY), F32),
            pltpu.VMEM((CZ, CHUNK, CY), F32),
            pltpu.VMEM((CZ + 1, CHUNK, CY), F32),
            pltpu.VMEM((CHUNKS, TFS, 3, CHUNK, CY), F32),
            pltpu.VMEM((CHUNKS, 4, 3, CHUNK, CY), F32),
            pltpu.VMEM((4, CHUNKS, 3, CHUNK, CY), F32),
            pltpu.SMEM((3,), F32),
            *[pltpu.SMEM((TFS,), F32)] * 4,
            pltpu.SMEM((3, TFS), F32),
            pltpu.VMEM((8, CY), F32),
            pltpu.VMEM((2 * CY, 2 * CY), BF16),
            pltpu.VMEM((CY, 2 * CY), BF16),
            pltpu.SemaphoreType.DMA((9,)),
            pltpu.SemaphoreType.DMA,
            pltpu.SemaphoreType.DMA((3, 2)),
            pltpu.SemaphoreType.DMA((3, 2)),
            pltpu.SemaphoreType.DMA((CHUNKS, 2)),
            pltpu.SemaphoreType.DMA((CHUNKS, 2)),
            pltpu.SemaphoreType.DMA((CHUNKS,)),
            pltpu.SemaphoreType.DMA((CHUNKS,)),
            pltpu.SemaphoreType.DMA((CHUNKS, 3)),
            pltpu.SemaphoreType.DMA((CHUNKS, 3)),
        ],
        compiler_params=pltpu.CompilerParams(collective_id=0, has_side_effects=True, vmem_limit_bytes=32 << 20),
        name="image",
    )(*operands)


def shards(depth_cell, column_cell, row_cell, mass, counts, diffusion, tf_center, tf_sharp, tf_opacity, tf_shade, tf_color):
    forth, back, back_low, cosine = (jnp.asarray(table) for table in tables())
    cells = [cell.reshape(128, 128) for cell in (depth_cell, column_cell, row_cell)]
    extended = deposit(counts, *cells, mass, forth)
    return image(
        diffusion, tf_center, tf_sharp, tf_opacity, tf_shade, tf_color.T, cosine, back, back_low, extended
    )


def solution(mesh):
    brick = P("depth", "cols", None)
    placed = (brick,) * 4 + (P("depth", "cols"),) + (P(),) * 6
    return jax.shard_map(shards, mesh=mesh, in_specs=placed, out_specs=brick, check_vma=False)
```

time: 62.3 us -> 52.8 us (0.85)
  Pallas kernels: 56 us -> 46.6 us
    pallas_call x1, Pallas kernels: 44.1 us -> 38.6 us  [image(): pl.pallas_call(image_kernel, out_shape=jax.ShapeDtypeStruct((4, CX, CY),...]
    pallas_call x1, Pallas kernels: 11.9 us -> 7.92 us  [deposit(): pl.pallas_call(deposit_kernel, out_shape=jax.ShapeDtypeStruct((CZ, PLANE,...]
where the time goes in v4:
time: 52.8 us; the launch traced here: 52.5 us
  Pallas kernels  46.6 us (88%)
  local copies, waits for them, and re-layouts  5.09 us (10%)
  between operations  0.85 us (2%)
    pallas_call x1, Pallas kernels, image(): pl.pallas_call(image_kernel, out_shape=jax.ShapeDtypeStruct((4, CX, CY),...  38.6 us
    pallas_call x1, Pallas kernels, deposit(): pl.pallas_call(deposit_kernel, out_shape=jax.ShapeDtypeStruct((CZ, PLANE,...  7.92 us
    unnamed x29, local copies, waits for them, and re-layouts  5.09 us

profile of v4, /device:TPU:1, one launch (start us, length us, event | category | flops | bytes accessed | tf_op | source)
XLA Modules:
  0.0 52.5 jit_solution(1053565782683959512)
XLA Ops:
  0.0 0.0 copy-start.7
  0.0 0.0 copy-start.8
  0.0 0.0 copy-start.13
  0.0 0.0 copy-start.12
  0.0 0.0 copy-start.11
  0.0 0.0 copy-start.10
  0.0 0.0 copy-start.9
  0.8 0.0 copy-start
  0.8 0.9 %copy-done = bf16[256,256]{1,0:T(8,128)(2,1)S(1)} copy-done((bf16[256,256]{1,0:T(8,128)(2,1)S(1)}, bf16[256,256]{1,0:T(8,128)(2,1)}, u32[]{:S(2)}) %copy-start) | copy-done | bytes 131096
  1.7 0.0 copy-start.2
  1.7 0.8 %copy-done.2 = s32[1,1,16384]{2,1,0:T(1,128)S(1)} copy-done((s32[1,1,16384]{2,1,0:T(1,128)S(1)}, s32[1,1,16384]{2,1,0:T(1,128)}, u32[]{:S(2)}) %copy-start.2) | copy-done | bytes 65560
  2.5 0.0 copy-start.3
  2.5 0.8 %copy-done.3 = s32[1,1,16384]{2,1,0:T(1,128)S(1)} copy-done((s32[1,1,16384]{2,1,0:T(1,128)S(1)}, s32[1,1,16384]{2,1,0:T(1,128)}, u32[]{:S(2)}) %copy-start.3) | copy-done | bytes 65560
  3.4 0.0 copy-start.4
  3.4 0.8 %copy-done.4 = s32[1,1,16384]{2,1,0:T(1,128)S(1)} copy-done((s32[1,1,16384]{2,1,0:T(1,128)S(1)}, s32[1,1,16384]{2,1,0:T(1,128)}, u32[]{:S(2)}) %copy-start.4) | copy-done | bytes 65560
  4.2 0.0 copy-start.5
  4.2 0.8 %copy-done.5 = bf16[1,1,16384]{2,1,0:T(2,128)(2,1)S(1)} copy-done((bf16[1,1,16384]{2,1,0:T(2,128)(2,1)S(1)}, bf16[1,1,16384]{2,1,0:T(2,128)(2,1)}, u32[]{:S(2)}) %copy-start.5) | copy-done | bytes 32792
  5.0 0.0 copy-start.1
  5.0 0.0 copy-start.6
  5.0 7.9 %deposit.1.ext = f32[16,288,128]{2,1,0:T(8,128)S(1)} custom-call(s32[1,1]{1,0:T(1,128)S(6)} %copy.17.count, s32[128,128]{1,0:T(8,128)S(1)} %bitcast.4, s32[128,128]{1,0:T(8,128)S(1)} %bitcast.5, s32[128,128]{1,0:T(8,128)S(1)} %bitcast.6, bf16[1,1,16384]{2,1,0:T(2,128)(2,1)S(1)} %copy-done.5, bf16[256,256]{1,0:T(8,128)(2,1)S(1)} %copy-done), custom_call_target="tpu_custom_call" | custom-call | tf_op jit(solution)/shard_map/deposit/pallas_call | solution.py:182
  13.0 0.0 copy-done.7
  13.0 0.0 copy-done.8
  13.0 0.0 copy-done.13
  13.0 0.0 copy-done.12
  13.0 0.0 copy-done.11
  13.0 0.0 copy-done.10
  13.0 0.0 copy-done.9
  13.0 0.0 copy-done.1
  13.0 0.0 copy-done.6
  13.1 38.6 %image.1 = f32[4,256,128]{2,1,0:T(8,128)S(1)} custom-call(f32[3]{0:T(128)S(1)} %copy-done.9, f32[8]{0:T(128)S(1)} %copy-done.10, f32[8]{0:T(128)S(1)} %copy-done.11, f32[8]{0:T(128)S(1)} %copy-done.12, f32[8]{0:T(128)S(1)} %copy-done.13, f32[3,8]{1,0:T(4,128)S(1)} %bitcast.7, f32[8,128]{1,0:T(8,128)S(1)} %copy-done.7, bf16[256,256]{1,0:T(8,128)(2,1)S(1)} %copy-done.1, ...), custom_call_target="tpu_custom_call" | custom-call | tf_op jit(solution)/shard_map/image/pallas_call | solution.py:477
  51.7 0.8 %copy.18 = f32[4,256,128]{2,1,0:T(8,128)} copy(f32[4,256,128]{2,1,0:T(8,128)S(1)} %image.1) | data formatting | bytes 1048576
Async XLA Ops:
  0.0 13.0 %copy-start.7 = (f32[8,128]{1,0:T(8,128)S(1)}, f32[8,128]{1,0:T(8,128)}, u32[]{:S(2)}) copy-start(f32[8,128]{1,0:T(8,128)} %constant.11.clone.cosine_h) | copy-start | bytes 12292
  0.0 13.0 %copy-start.8 = (f32[8,3]{0,1:T(4,128)S(1)}, f32[8,3]{0,1:T(4,128)}, u32[]{:S(2)}) copy-start(f32[8,3]{0,1:T(4,128)} %param.25) | copy-start | bytes 292
  0.0 13.0 %copy-start.13 = (f32[8]{0:T(128)S(1)}, f32[8]{0:T(128)}, u32[]{:S(2)}) copy-start(f32[8]{0:T(128)} %shade_h.1) | copy-start | bytes 100
  0.0 13.0 %copy-start.12 = (f32[8]{0:T(128)S(1)}, f32[8]{0:T(128)}, u32[]{:S(2)}) copy-start(f32[8]{0:T(128)} %tfo_h.1) | copy-start | bytes 100
  0.0 13.0 %copy-start.11 = (f32[8]{0:T(128)S(1)}, f32[8]{0:T(128)}, u32[]{:S(2)}) copy-start(f32[8]{0:T(128)} %tfs_h.1) | copy-start | bytes 100
  0.0 13.0 %copy-start.10 = (f32[8]{0:T(128)S(1)}, f32[8]{0:T(128)}, u32[]{:S(2)}) copy-start(f32[8]{0:T(128)} %tfc_h.1) | copy-start | bytes 100
  0.0 13.0 %copy-start.9 = (f32[3]{0:T(128)S(1)}, f32[3]{0:T(128)}, u32[]{:S(2)}) copy-start(f32[3]{0:T(128)} %dif_h.1) | copy-start | bytes 40
  0.8 0.9 %copy-start = (bf16[256,256]{1,0:T(8,128)(2,1)S(1)}, bf16[256,256]{1,0:T(8,128)(2,1)}, u32[]{:S(2)}) copy-start(bf16[256,256]{1,0:T(8,128)(2,1)} %constant.8.clone.fh) | copy-start | bytes 393220
  1.7 0.8 %copy-start.2 = (s32[1,1,16384]{2,1,0:T(1,128)S(1)}, s32[1,1,16384]{2,1,0:T(1,128)}, u32[]{:S(2)}) copy-start(s32[1,1,16384]{2,1,0:T(1,128)} %param.15) | copy-start | bytes 196612
  2.5 0.8 %copy-start.3 = (s32[1,1,16384]{2,1,0:T(1,128)S(1)}, s32[1,1,16384]{2,1,0:T(1,128)}, u32[]{:S(2)}) copy-start(s32[1,1,16384]{2,1,0:T(1,128)} %param.16) | copy-start | bytes 196612
  3.4 0.8 %copy-start.4 = (s32[1,1,16384]{2,1,0:T(1,128)S(1)}, s32[1,1,16384]{2,1,0:T(1,128)}, u32[]{:S(2)}) copy-start(s32[1,1,16384]{2,1,0:T(1,128)} %param.17) | copy-start | bytes 196612
  4.2 0.8 %copy-start.5 = (bf16[1,1,16384]{2,1,0:T(2,128)(2,1)S(1)}, bf16[1,1,16384]{2,1,0:T(2,128)(2,1)}, u32[]{:S(2)}) copy-start(bf16[1,1,16384]{2,1,0:T(2,128)(2,1)} %mh.1) | copy-start | bytes 98308
  5.0 8.0 %copy-start.1 = (bf16[256,256]{1,0:T(8,128)(2,1)S(1)}, bf16[256,256]{1,0:T(8,128)(2,1)}, u32[]{:S(2)}) copy-start(bf16[256,256]{1,0:T(8,128)(2,1)} %constant.9.clone.back_h) | copy-start | bytes 393220
  5.0 8.0 %copy-start.6 = (bf16[128,256]{1,0:T(8,128)(2,1)S(1)}, bf16[128,256]{1,0:T(8,128)(2,1)}, u32[]{:S(2)}) copy-start(bf16[128,256]{1,0:T(8,128)(2,1)} %constant.10.clone.low_h) | copy-start | bytes 196612

commit v5 on v4

--- a/solution.py
+++ b/solution.py
@@ -287,14 +287,16 @@
     chips = nd // 2
     partner = (depth + 1 - 2 * core, cols)
 
-    def beside(dz, dx):
-        return ((depth + dz + nd) % nd, (cols + dx + nc) % nc)
-
+    exists = {(-1, 0): depth > 0, (1, 0): depth < nd - 1, (0, -1): cols > 0, (0, 1): cols < nc - 1}
     barrier = pltpu.get_barrier_semaphore()
-    friends = [beside(-1, 0), beside(1, 0), beside(0, -1), beside(0, 1)]
-    friends += [((depth + 2 * n) % nd, cols) for n in range(1, chips)]
-    for friend in friends:
-        pl.semaphore_signal(barrier, inc=1, device_id=friend, device_id_type=MESH)
+
+    def greet(device):
+        pl.semaphore_signal(barrier, inc=1, device_id=device, device_id_type=MESH)
+
+    for dz, dx in exists:
+        pl.when(exists[dz, dx])(functools.partial(greet, (depth + dz, cols + dx)))
+    for n in range(1, chips):
+        greet(((depth + 2 * n) % nd, cols))
     pairs = (
         (dif_h, dif), (tfc_h, tfc), (tfs_h, tfs), (tfo_h, tfo), (shade_h, shade), (tint_h, tint),
         (cosine_h, cosine), (back_h, back), (low_h, back_low),
@@ -315,38 +317,77 @@
     for z in (*range(HALO), *range(HALO + CZ, DEEP)):
         one[z, 0:8, :] = zeros
         one[z, 280:288, :] = zeros
-    pl.semaphore_wait(barrier, len(friends))
+
+    def clear(ref, first, begin, rows):
+        @pl.when(depth == 0)
+        def _():
+            for z in range(first, HALO):
+                ref[z, begin : begin + rows, :] = jnp.zeros((rows, CY), F32)
+
+        @pl.when(depth == nd - 1)
+        def _():
+            for z in range(HALO + CZ, DEEP - first):
+                ref[z, begin : begin + rows, :] = jnp.zeros((rows, CY), F32)
+
+    clear(one, 0, 8, 272)
+
+    @pl.when(cols == 0)
+    def _():
+        left[...] = jnp.zeros((DEEP, 16, CY), F32)
+
+    @pl.when(cols == nc - 1)
+    def _():
+        right[...] = jnp.zeros((DEEP, 16, CY), F32)
+
+    pl.semaphore_wait(barrier, sum(near.astype(jnp.int32) for near in exists.values()) + chips - 1)
 
     planes = {1: (CZ - HALO, 0, HALO), -1: (0, HALO + CZ, HALO)}
 
-    def copy_to(source, target, send, recv, device):
-        copy = pltpu.make_async_remote_copy(
+    def copy_of(source, target, send, recv, device):
+        return pltpu.make_async_remote_copy(
             src_ref=source, dst_ref=target, send_sem=send, recv_sem=recv, device_id=device, device_id_type=MESH
         )
-        copy.start()
-        return copy
-
-    halos, sides = [], []
-
-    def send_side(n, source, begin, count, at):
+
+    def halo(step, dz, act):
+        begin, rows = PARTS[step]
+        src, dst, count = planes[dz]
+        n = (1 + dz) // 2
+        copy = copy_of(
+            ext.at[pl.ds(src, count), pl.ds(begin, rows)], one.at[pl.ds(dst, count), pl.ds(begin, rows)],
+            halo_send.at[step, n], halo_recv.at[step, n], (depth + dz, cols),
+        )
+        pl.when(exists[dz, 0])(lambda: getattr(copy, act)())
+
+    def start_halo(step):
+        for dz in (-1, 1):
+            halo(step, dz, "start")
+
+    def arrive(step):
+        for dz in (-1, 1):
+            halo(step, dz, "wait_send")
+            begin, rows = PARTS[step]
+            src, dst, count = planes[dz]
+            n = (1 + dz) // 2
+            copy = copy_of(
+                ext.at[pl.ds(src, count), pl.ds(begin, rows)], one.at[pl.ds(dst, count), pl.ds(begin, rows)],
+                halo_send.at[step, n], halo_recv.at[step, n], (depth - dz, cols),
+            )
+            pl.when(exists[-dz, 0])(copy.wait_recv)
+
+    spots = ((0, CZ, HALO), (0, HALO, 0), (HALO + CZ, HALO, HALO + CZ))
+
+    def side(n, act):
+        begin, count, at = spots[n]
+        source = one if n else ext
         for m, dx, target in ((0, 1, left), (1, -1, right)):
-            sides.append(
-                copy_to(
-                    source.at[pl.ds(begin, count), pl.ds(264 if dx == 1 else 8, 16)], target.at[pl.ds(at, count)],
-                    side_send.at[n, m], side_recv.at[n, m], beside(0, dx),
-                )
+            copy = copy_of(
+                source.at[pl.ds(begin, count), pl.ds(264 if dx == 1 else 8, 16)], target.at[pl.ds(at, count)],
+                side_send.at[n, m], side_recv.at[n, m], (depth, cols + dx),
             )
-
-    for step, (begin, rows) in enumerate(PARTS):
-        for n, dz in enumerate((-1, 1)):
-            src, dst, count = planes[dz]
-            halos.append(
-                copy_to(
-                    ext.at[pl.ds(src, count), pl.ds(begin, rows)], one.at[pl.ds(dst, count), pl.ds(begin, rows)],
-                    halo_send.at[step, n], halo_recv.at[step, n], beside(dz, 0),
-                )
-            )
-    send_side(0, ext, 0, CZ, HALO)
+            pl.when(exists[0, dx] if act != "wait_recv" else exists[0, -dx])(lambda: getattr(copy, act)())
+
+    start_halo(0)
+    side(0, "start")
     inner.wait()
     for load in loads:
         load.wait()
@@ -359,21 +400,6 @@
     ratio = jnp.full((8, CY), d1, F32) / along
     square = d0 * d0
 
-    def clear(ref, first, begin, rows):
-        @pl.when(depth == 0)
-        def _():
-            for z in range(first, HALO):
-                ref[z, begin : begin + rows, :] = jnp.zeros((rows, CY), F32)
-
-        @pl.when(depth == nd - 1)
-        def _():
-            for z in range(HALO + CZ, DEEP - first):
-                ref[z, begin : begin + rows, :] = jnp.zeros((rows, CY), F32)
-
-    def arrive(step):
-        for halo in halos[2 * step : 2 * step + 2]:
-            halo.wait()
-
     def draw(chunk, own):
         @pl.loop(0, chips)
         def _(j):
@@ -381,12 +407,19 @@
             sharp = 0.5 * tfs[k]
             out_ref = mine.at[chunk, j + (chips if own else 0)]
             render(ta, rise_d, rise_g, out_ref, sharp, -sharp * tfc[k], 0.5 * tfo[k])
-
-    swaps, sends = {}, []
+            if not own:
+                swap_of(chunk, j).start()
+
+    def swap_of(chunk, j):
+        return copy_of(
+            mine.at[chunk, j], came.at[chunk, j], pair_send.at[chunk, j], pair_recv.at[chunk, j], partner
+        )
+
+    sends = []
 
     def combine(chunk):
-        swaps[chunk].wait_recv()
-        for j in range(chips):
+        for j in (0, 1, 3, 2):
+            swap_of(chunk, j).wait_recv()
             i = (chip + j + 2) % chips
             held = mine.at[chunk, chips + j]
             place = whole.at[chip, chunk] if j == 2 else held
@@ -399,21 +432,23 @@
                 place[2, at, :] = first[2] * then[2]
             if j != 2:
                 m = j - j // 3
-                sends.append(
-                    copy_to(
-                        held, whole.at[chip, chunk], far_send.at[chunk, m], far_recv.at[chunk, m],
-                        (2 * i + core, cols),
-                    )
+                send = copy_of(
+                    held, whole.at[chip, chunk], far_send.at[chunk, m], far_recv.at[chunk, m], (2 * i + core, cols)
                 )
+                send.start()
+                sends.append(send)
 
     for step in range(CHUNKS):
         chunk = ORDER[step]
         if step < 2:
             arrive(step)
-            clear(one, 0, *PARTS[step])
+        if step == 0:
+            for later in range(1, CHUNKS):
+                start_halo(later)
         if step == 2:
-            for side in sides:
-                side.wait()
+            for n in range(3):
+                side(n, "wait_send")
+                side(n, "wait_recv")
 
             @pl.loop(0, DEEP)
             def _(z):
@@ -421,9 +456,6 @@
                 one[z, 16:24, :] = one[z, 16:24, :] + left[z, 8:16, :] * has_left
                 one[z, 264:272, :] = one[z, 264:272, :] + right[z, 0:8, :] * has_right
                 one[z, 272:280, :] = (one[z, 272:280, :] + right[z, 8:16, :]) * has_right
-
-            clear(one, 0, *PARTS[2])
-            clear(one, 0, *PARTS[3])
         x_live = {0: has_left} if chunk == 0 else {SPAN // 8 - 1: has_right} if chunk == CHUNKS - 1 else {}
         sweep(one, 8 + CHUNK * chunk, ta, 1, DEEP - 1, 8, center, ratio, x_live)
         clear(ta, 1, 8, SPAN)
@@ -438,14 +470,11 @@
         if step == 1:
             arrive(2)
             arrive(3)
-            send_side(1, one, 0, HALO, 0)
-            send_side(2, one, HALO + CZ, HALO, HALO + CZ)
+            side(1, "start")
+            side(2, "start")
         back_to_cells(tb, ta, grad, back, back_low, square * square)
         gradient(ta, grad, rise_d, rise_g)
         draw(chunk, False)
-        swaps[chunk] = copy_to(
-            mine.at[chunk, pl.ds(0, chips)], came.at[chunk], pair_send.at[chunk], pair_recv.at[chunk], partner
-        )
         draw(chunk, True)
     combine(ORDER[-1])
 
@@ -468,7 +497,8 @@
                 out[q, to, :] = sum_d * color[q] + sum_g * shading
             out[3, to, :] = keep
     for chunk in ORDER:
-        swaps[chunk].wait_send()
+        for j in range(chips):
+            swap_of(chunk, j).wait_send()
 
 
 def image(*operands):
@@ -503,8 +533,8 @@
             pltpu.SemaphoreType.DMA((3, 2)),
             pltpu.SemaphoreType.DMA((CHUNKS, 2)),
             pltpu.SemaphoreType.DMA((CHUNKS, 2)),
-            pltpu.SemaphoreType.DMA((CHUNKS,)),
-            pltpu.SemaphoreType.DMA((CHUNKS,)),
+            pltpu.SemaphoreType.DMA((CHUNKS, 4)),
+            pltpu.SemaphoreType.DMA((CHUNKS, 4)),
             pltpu.SemaphoreType.DMA((CHUNKS, 3)),
             pltpu.SemaphoreType.DMA((CHUNKS, 3)),
         ],
@@ -516,7 +546,7 @@
 def shards(depth_cell, column_cell, row_cell, mass, counts, diffusion, tf_center, tf_sharp, tf_opacity, tf_shade, tf_color):
     forth, back, back_low, cosine = (jnp.asarray(table) for table in tables())
     cells = [cell.reshape(128, 128) for cell in (depth_cell, column_cell, row_cell)]
-    extended = deposit(counts, *cells, mass, forth)
+    extended = deposit(counts, *(pltpu.with_memory_space_constraint(x, pltpu.HBM) for x in (*cells, mass, forth)))
     return image(
         diffusion, tf_center, tf_sharp, tf_opacity, tf_shade, tf_color.T, cosine, back, back_low, extended
     )

time: 52.8 us -> 49.9 us (0.945)
  the two profiles are of different devices: /device:TPU:1 before, /device:TPU:6 now
where the time goes in v5:
time: 49.9 us; the launch traced here: 49.7 us
  Pallas kernels  48 us (96%)
  between operations  0.93 us (2%)
  local copies, waits for them, and re-layouts  0.83 us (2%)
    pallas_call x1, Pallas kernels, image(): pl.pallas_call(image_kernel, out_shape=jax.ShapeDtypeStruct((4, CX, CY),...  39.7 us
    pallas_call x1, Pallas kernels, deposit(): pl.pallas_call(deposit_kernel, out_shape=jax.ShapeDtypeStruct((CZ, PLANE,...  8.25 us

profile of v5, /device:TPU:6, one launch (start us, length us, event | category | flops | bytes accessed | tf_op | source)
XLA Modules:
  0.0 49.7 jit_solution(1683767916760209870)
XLA Ops:
  0.0 0.0 copy-start.2
  0.0 0.0 copy-start.1
  0.0 0.0 copy-start
  0.0 0.0 copy-start.3
  0.0 0.0 copy-start.8
  0.0 0.0 copy-start.7
  0.0 0.0 copy-start.6
  0.0 0.0 copy-start.5
  0.1 0.0 copy-start.4
  0.9 8.3 %deposit.1.ext = f32[16,288,128]{2,1,0:T(8,128)S(1)} custom-call(s32[1,1]{1,0:T(1,128)S(6)} %copy.17.count, s32[128,128]{1,0:T(8,128)} %bitcast.5, s32[128,128]{1,0:T(8,128)} %bitcast.6, s32[128,128]{1,0:T(8,128)} %bitcast.7, bf16[1,1,16384]{2,1,0:T(2,128)(2,1)} %mh.1, bf16[256,256]{1,0:T(8,128)(2,1)} %constant.8.clone.fh), custom_call_target="tpu_custom_call" | custom-call | tf_op jit(solution)/shard_map/deposit/pallas_call | solution.py:182
  9.1 0.0 copy-done.2
  9.1 0.0 copy-done.1
  9.1 0.0 copy-done
  9.1 0.0 copy-done.3
  9.2 0.0 copy-done.8
  9.2 0.0 copy-done.7
  9.2 0.0 copy-done.6
  9.2 0.0 copy-done.5
  9.2 0.0 copy-done.4
  9.2 39.7 %image.1 = f32[4,256,128]{2,1,0:T(8,128)S(1)} custom-call(f32[3]{0:T(128)S(1)} %copy-done.4, f32[8]{0:T(128)S(1)} %copy-done.5, f32[8]{0:T(128)S(1)} %copy-done.6, f32[8]{0:T(128)S(1)} %copy-done.7, f32[8]{0:T(128)S(1)} %copy-done.8, f32[3,8]{1,0:T(4,128)S(1)} %bitcast.4, f32[8,128]{1,0:T(8,128)S(1)} %copy-done.2, bf16[256,256]{1,0:T(8,128)(2,1)S(1)} %copy-done, ...), custom_call_target="tpu_custom_call" | custom-call | tf_op jit(solution)/shard_map/image/pallas_call | solution.py:507
  48.9 0.8 %copy.18 = f32[4,256,128]{2,1,0:T(8,128)} copy(f32[4,256,128]{2,1,0:T(8,128)S(1)} %image.1) | data formatting | bytes 1048576
Async XLA Ops:
  0.0 9.1 %copy-start.2 = (f32[8,128]{1,0:T(8,128)S(1)}, f32[8,128]{1,0:T(8,128)}, u32[]{:S(2)}) copy-start(f32[8,128]{1,0:T(8,128)} %constant.11.clone.cosine_h) | copy-start | bytes 12292
  0.0 9.1 %copy-start.1 = (bf16[128,256]{1,0:T(8,128)(2,1)S(1)}, bf16[128,256]{1,0:T(8,128)(2,1)}, u32[]{:S(2)}) copy-start(bf16[128,256]{1,0:T(8,128)(2,1)} %constant.10.clone.low_h) | copy-start | bytes 196612
  0.0 9.1 %copy-start = (bf16[256,256]{1,0:T(8,128)(2,1)S(1)}, bf16[256,256]{1,0:T(8,128)(2,1)}, u32[]{:S(2)}) copy-start(bf16[256,256]{1,0:T(8,128)(2,1)} %constant.9.clone.back_h) | copy-start | bytes 393220
  0.0 9.1 %copy-start.3 = (f32[8,3]{0,1:T(4,128)S(1)}, f32[8,3]{0,1:T(4,128)}, u32[]{:S(2)}) copy-start(f32[8,3]{0,1:T(4,128)} %param.25) | copy-start | bytes 292
  0.0 9.1 %copy-start.8 = (f32[8]{0:T(128)S(1)}, f32[8]{0:T(128)}, u32[]{:S(2)}) copy-start(f32[8]{0:T(128)} %shade_h.1) | copy-start | bytes 100
  0.0 9.1 %copy-start.7 = (f32[8]{0:T(128)S(1)}, f32[8]{0:T(128)}, u32[]{:S(2)}) copy-start(f32[8]{0:T(128)} %tfo_h.1) | copy-start | bytes 100
  0.0 9.1 %copy-start.6 = (f32[8]{0:T(128)S(1)}, f32[8]{0:T(128)}, u32[]{:S(2)}) copy-start(f32[8]{0:T(128)} %tfs_h.1) | copy-start | bytes 100
  0.0 9.1 %copy-start.5 = (f32[8]{0:T(128)S(1)}, f32[8]{0:T(128)}, u32[]{:S(2)}) copy-start(f32[8]{0:T(128)} %tfc_h.1) | copy-start | bytes 100
  0.1 9.1 %copy-start.4 = (f32[3]{0:T(128)S(1)}, f32[3]{0:T(128)}, u32[]{:S(2)}) copy-start(f32[3]{0:T(128)} %dif_h.1) | copy-start | bytes 40

commit v6 on v5

--- a/solution.py
+++ b/solution.py
@@ -388,6 +388,8 @@
 
     start_halo(0)
     side(0, "start")
+    for later in range(1, CHUNKS):
+        start_halo(later)
     inner.wait()
     for load in loads:
         load.wait()
@@ -442,9 +444,6 @@
         chunk = ORDER[step]
         if step < 2:
             arrive(step)
-        if step == 0:
-            for later in range(1, CHUNKS):
-                start_halo(later)
         if step == 2:
             for n in range(3):
                 side(n, "wait_send")

time: 49.9 us -> 45.4 us (0.910)
  Pallas kernels: 48 us -> 43.5 us
    pallas_call x1, Pallas kernels: 39.7 us -> 35.2 us  [image(): pl.pallas_call(image_kernel, out_shape=jax.ShapeDtypeStruct((4, CX, CY),...]
where the time goes in v6:
time: 45.4 us; the launch traced here: 45.2 us
  Pallas kernels  43.5 us (96%)
  between operations  0.93 us (2%)
  local copies, waits for them, and re-layouts  0.83 us (2%)
    pallas_call x1, Pallas kernels, image(): pl.pallas_call(image_kernel, out_shape=jax.ShapeDtypeStruct((4, CX, CY),...  35.2 us
    pallas_call x1, Pallas kernels, deposit(): pl.pallas_call(deposit_kernel, out_shape=jax.ShapeDtypeStruct((CZ, PLANE,...  8.25 us

profile of v6, /device:TPU:6, one launch (start us, length us, event | category | flops | bytes accessed | tf_op | source)
XLA Modules:
  0.0 45.2 jit_solution(1488920214355042462)
XLA Ops:
  0.0 0.0 copy-start.2
  0.0 0.0 copy-start.1
  0.0 0.0 copy-start
  0.0 0.0 copy-start.3
  0.0 0.0 copy-start.8
  0.0 0.0 copy-start.7
  0.0 0.0 copy-start.6
  0.0 0.0 copy-start.5
  0.1 0.0 copy-start.4
  0.9 8.3 %deposit.1.ext = f32[16,288,128]{2,1,0:T(8,128)S(1)} custom-call(s32[1,1]{1,0:T(1,128)S(6)} %copy.17.count, s32[128,128]{1,0:T(8,128)} %bitcast.5, s32[128,128]{1,0:T(8,128)} %bitcast.6, s32[128,128]{1,0:T(8,128)} %bitcast.7, bf16[1,1,16384]{2,1,0:T(2,128)(2,1)} %mh.1, bf16[256,256]{1,0:T(8,128)(2,1)} %constant.8.clone.fh), custom_call_target="tpu_custom_call" | custom-call | tf_op jit(solution)/shard_map/deposit/pallas_call | solution.py:182
  9.1 0.0 copy-done.2
  9.1 0.0 copy-done.1
  9.1 0.0 copy-done
  9.1 0.0 copy-done.3
  9.2 0.0 copy-done.8
  9.2 0.0 copy-done.7
  9.2 0.0 copy-done.6
  9.2 0.0 copy-done.5
  9.2 0.0 copy-done.4
  9.2 35.2 %image.1 = f32[4,256,128]{2,1,0:T(8,128)S(1)} custom-call(f32[3]{0:T(128)S(1)} %copy-done.4, f32[8]{0:T(128)S(1)} %copy-done.5, f32[8]{0:T(128)S(1)} %copy-done.6, f32[8]{0:T(128)S(1)} %copy-done.7, f32[8]{0:T(128)S(1)} %copy-done.8, f32[3,8]{1,0:T(4,128)S(1)} %bitcast.4, f32[8,128]{1,0:T(8,128)S(1)} %copy-done.2, bf16[256,256]{1,0:T(8,128)(2,1)S(1)} %copy-done, ...), custom_call_target="tpu_custom_call" | custom-call | tf_op jit(solution)/shard_map/image/pallas_call | solution.py:506
  44.4 0.8 %copy.18 = f32[4,256,128]{2,1,0:T(8,128)} copy(f32[4,256,128]{2,1,0:T(8,128)S(1)} %image.1) | data formatting | bytes 1048576
Async XLA Ops:
  0.0 9.1 %copy-start.2 = (f32[8,128]{1,0:T(8,128)S(1)}, f32[8,128]{1,0:T(8,128)}, u32[]{:S(2)}) copy-start(f32[8,128]{1,0:T(8,128)} %constant.11.clone.cosine_h) | copy-start | bytes 12292
  0.0 9.1 %copy-start.1 = (bf16[128,256]{1,0:T(8,128)(2,1)S(1)}, bf16[128,256]{1,0:T(8,128)(2,1)}, u32[]{:S(2)}) copy-start(bf16[128,256]{1,0:T(8,128)(2,1)} %constant.10.clone.low_h) | copy-start | bytes 196612
  0.0 9.1 %copy-start = (bf16[256,256]{1,0:T(8,128)(2,1)S(1)}, bf16[256,256]{1,0:T(8,128)(2,1)}, u32[]{:S(2)}) copy-start(bf16[256,256]{1,0:T(8,128)(2,1)} %constant.9.clone.back_h) | copy-start | bytes 393220
  0.0 9.1 %copy-start.3 = (f32[8,3]{0,1:T(4,128)S(1)}, f32[8,3]{0,1:T(4,128)}, u32[]{:S(2)}) copy-start(f32[8,3]{0,1:T(4,128)} %param.25) | copy-start | bytes 292
  0.0 9.1 %copy-start.8 = (f32[8]{0:T(128)S(1)}, f32[8]{0:T(128)}, u32[]{:S(2)}) copy-start(f32[8]{0:T(128)} %shade_h.1) | copy-start | bytes 100
  0.0 9.1 %copy-start.7 = (f32[8]{0:T(128)S(1)}, f32[8]{0:T(128)}, u32[]{:S(2)}) copy-start(f32[8]{0:T(128)} %tfo_h.1) | copy-start | bytes 100
  0.0 9.1 %copy-start.6 = (f32[8]{0:T(128)S(1)}, f32[8]{0:T(128)}, u32[]{:S(2)}) copy-start(f32[8]{0:T(128)} %tfs_h.1) | copy-start | bytes 100
  0.0 9.1 %copy-start.5 = (f32[8]{0:T(128)S(1)}, f32[8]{0:T(128)}, u32[]{:S(2)}) copy-start(f32[8]{0:T(128)} %tfc_h.1) | copy-start | bytes 100
  0.1 9.1 %copy-start.4 = (f32[3]{0:T(128)S(1)}, f32[3]{0:T(128)}, u32[]{:S(2)}) copy-start(f32[3]{0:T(128)} %dif_h.1) | copy-start | bytes 40

commit v7 on v6

--- a/solution.py
+++ b/solution.py
@@ -16,7 +16,7 @@
 XO = 16
 ROWS = CZ * PLANE
 WIN = 112
-UNROLL = 8
+UNROLL = 32
 SLOTS = 16384
 NBLK = SLOTS // 256
 MESH = pl.DeviceIdType.MESH
@@ -123,8 +123,9 @@
         raw[8 * i : 8 * i + 8, :] = keys[i]
     tidy[...] = raw[...].T
     found.wait()
-    ys = lax.broadcasted_iota(jnp.int32, (128, 128), 0)
-    ws = lax.broadcasted_iota(jnp.int32, (WIN, 128), 0)
+    ys = lax.broadcasted_iota(jnp.int32, (128, 128), 0).astype(F32).astype(BF16)
+    ws = lax.broadcasted_iota(jnp.int32, (WIN, 128), 0).astype(F32).astype(BF16)
+    one, none = jnp.ones((), BF16), jnp.zeros((), BF16)
 
     def block(b, start, begin):
         hots, y_hots = [], []
@@ -133,9 +134,9 @@
             row = (key >> 19) + 4096
             if begin is not None:
                 row = jnp.where(row >= begin, row, -1)
-            hots.append(jnp.where(ws == row - start, 1.0, 0.0).astype(BF16))
-            weight = (key & 4095).astype(F32) * (1.0 / 64.0)
-            y_hots.append(jnp.where(ys == ((key >> 12) & 127), weight, 0.0).astype(BF16))
+            hots.append(jnp.where(ws == (row - start).astype(F32).astype(BF16), one, none))
+            weight = ((key & 4095).astype(F32) * (1.0 / 64.0)).astype(BF16)
+            y_hots.append(jnp.where(ys == ((key >> 12) & 127).astype(F32).astype(BF16), weight, none))
         hot, y_hot = jnp.concatenate(hots, axis=1), jnp.concatenate(y_hots, axis=1)
         return lax.dot_general(hot, y_hot, (((1,), (1,)), ((), ())), preferred_element_type=F32)
 
@@ -170,11 +171,8 @@
                     place = pl.multiple_of(jnp.minimum(begin, ROWS - WIN), 8)
                     acc[pl.ds(place, WIN), :] += block(b, place, begin)
 
-    @pl.loop(0, CZ // 4)
-    def _(step):
-        rows = acc[pl.ds(pl.multiple_of(step * (4 * PLANE), 8), 4 * PLANE), :]
-        both = jnp.dot(jnp.concatenate(pair_of(rows), axis=1), forth[...], preferred_element_type=F32)
-        out[pl.ds(step * 4, 4)] = (both[:, :CY] + both[:, CY:]).reshape(4, PLANE, CY)
+    both = jnp.dot(jnp.concatenate(pair_of(acc[...]), axis=1), forth[...], preferred_element_type=F32)
+    out[...] = (both[:, :CY] + both[:, CY:]).reshape(CZ, PLANE, CY)
 
 
 def deposit(count, zc, xc, yc, mass, forth):
@@ -442,9 +440,9 @@
 
     for step in range(CHUNKS):
         chunk = ORDER[step]
-        if step < 2:
+        if step < CHUNKS - 2:
             arrive(step)
-        if step == 2:
+        if step == CHUNKS - 2:
             for n in range(3):
                 side(n, "wait_send")
                 side(n, "wait_recv")
@@ -458,17 +456,17 @@
         x_live = {0: has_left} if chunk == 0 else {SPAN // 8 - 1: has_right} if chunk == CHUNKS - 1 else {}
         sweep(one, 8 + CHUNK * chunk, ta, 1, DEEP - 1, 8, center, ratio, x_live)
         clear(ta, 1, 8, SPAN)
+        if step:
+            combine(ORDER[step - 1])
         sweep(ta, 8, tb, 2, DEEP - 2, 11, center, ratio, x_live)
         clear(tb, 2, 8, SPAN)
-        if step:
-            combine(ORDER[step - 1])
         sweep(tb, 8, ta, 3, DEEP - 3, 10, center, ratio, x_live)
         clear(ta, 3, 8, SPAN)
         sweep(ta, 8, tb, 4, DEEP - 4, 9, center, ratio, x_live)
         clear(tb, 4, 8, SPAN)
-        if step == 1:
-            arrive(2)
-            arrive(3)
+        if step == CHUNKS // 2 - 1:
+            arrive(CHUNKS - 2)
+            arrive(CHUNKS - 1)
             side(1, "start")
             side(2, "start")
         back_to_cells(tb, ta, grad, back, back_low, square * square)

time: 45.4 us -> 43.5 us (0.958)
  Pallas kernels: 43.5 us -> 41.6 us
    pallas_call x1, Pallas kernels: 8.25 us -> 6.63 us  [deposit(): pl.pallas_call(deposit_kernel, out_shape=jax.ShapeDtypeStruct((CZ, PLANE,...]
where the time goes in v7:
time: 43.5 us; the launch traced here: 43.3 us
  Pallas kernels  41.6 us (96%)
  between operations  0.93 us (2%)
  local copies, waits for them, and re-layouts  0.83 us (2%)
    pallas_call x1, Pallas kernels, image(): pl.pallas_call(image_kernel, out_shape=jax.ShapeDtypeStruct((4, CX, CY),...  34.9 us
    pallas_call x1, Pallas kernels, deposit(): pl.pallas_call(deposit_kernel, out_shape=jax.ShapeDtypeStruct((CZ, PLANE,...  6.63 us

profile of v7, /device:TPU:6, one launch (start us, length us, event | category | flops | bytes accessed | tf_op | source)
XLA Modules:
  0.0 43.3 jit_solution(9834234674646429318)
XLA Ops:
  0.0 0.0 copy-start.2
  0.0 0.0 copy-start.1
  0.0 0.0 copy-start
  0.0 0.0 copy-start.3
  0.0 0.0 copy-start.8
  0.0 0.0 copy-start.7
  0.0 0.0 copy-start.6
  0.0 0.0 copy-start.5
  0.1 0.0 copy-start.4
  0.9 6.6 %deposit.1.ext = f32[16,288,128]{2,1,0:T(8,128)S(1)} custom-call(s32[1,1]{1,0:T(1,128)S(6)} %copy.17.count, s32[128,128]{1,0:T(8,128)} %bitcast.5, s32[128,128]{1,0:T(8,128)} %bitcast.6, s32[128,128]{1,0:T(8,128)} %bitcast.7, bf16[1,1,16384]{2,1,0:T(2,128)(2,1)} %mh.1, bf16[256,256]{1,0:T(8,128)(2,1)} %constant.8.clone.fh), custom_call_target="tpu_custom_call" | custom-call | tf_op jit(solution)/shard_map/deposit/pallas_call | solution.py:180
  7.5 0.0 copy-done.2
  7.5 0.0 copy-done.1
  7.5 0.0 copy-done
  7.5 0.0 copy-done.3
  7.5 0.0 copy-done.8
  7.5 0.0 copy-done.7
  7.5 0.0 copy-done.6
  7.6 0.0 copy-done.5
  7.6 0.0 copy-done.4
  7.6 34.9 %image.1 = f32[4,256,128]{2,1,0:T(8,128)S(1)} custom-call(f32[3]{0:T(128)S(1)} %copy-done.4, f32[8]{0:T(128)S(1)} %copy-done.5, f32[8]{0:T(128)S(1)} %copy-done.6, f32[8]{0:T(128)S(1)} %copy-done.7, f32[8]{0:T(128)S(1)} %copy-done.8, f32[3,8]{1,0:T(4,128)S(1)} %bitcast.4, f32[8,128]{1,0:T(8,128)S(1)} %copy-done.2, bf16[256,256]{1,0:T(8,128)(2,1)S(1)} %copy-done, ...), custom_call_target="tpu_custom_call" | custom-call | tf_op jit(solution)/shard_map/image/pallas_call | solution.py:504
  42.5 0.8 %copy.18 = f32[4,256,128]{2,1,0:T(8,128)} copy(f32[4,256,128]{2,1,0:T(8,128)S(1)} %image.1) | data formatting | bytes 1048576
Async XLA Ops:
  0.0 7.5 %copy-start.2 = (f32[8,128]{1,0:T(8,128)S(1)}, f32[8,128]{1,0:T(8,128)}, u32[]{:S(2)}) copy-start(f32[8,128]{1,0:T(8,128)} %constant.11.clone.cosine_h) | copy-start | bytes 12292
  0.0 7.5 %copy-start.1 = (bf16[128,256]{1,0:T(8,128)(2,1)S(1)}, bf16[128,256]{1,0:T(8,128)(2,1)}, u32[]{:S(2)}) copy-start(bf16[128,256]{1,0:T(8,128)(2,1)} %constant.10.clone.low_h) | copy-start | bytes 196612
  0.0 7.5 %copy-start = (bf16[256,256]{1,0:T(8,128)(2,1)S(1)}, bf16[256,256]{1,0:T(8,128)(2,1)}, u32[]{:S(2)}) copy-start(bf16[256,256]{1,0:T(8,128)(2,1)} %constant.9.clone.back_h) | copy-start | bytes 393220
  0.0 7.5 %copy-start.3 = (f32[8,3]{0,1:T(4,128)S(1)}, f32[8,3]{0,1:T(4,128)}, u32[]{:S(2)}) copy-start(f32[8,3]{0,1:T(4,128)} %param.25) | copy-start | bytes 292
  0.0 7.5 %copy-start.8 = (f32[8]{0:T(128)S(1)}, f32[8]{0:T(128)}, u32[]{:S(2)}) copy-start(f32[8]{0:T(128)} %shade_h.1) | copy-start | bytes 100
  0.0 7.5 %copy-start.7 = (f32[8]{0:T(128)S(1)}, f32[8]{0:T(128)}, u32[]{:S(2)}) copy-start(f32[8]{0:T(128)} %tfo_h.1) | copy-start | bytes 100
  0.0 7.5 %copy-start.6 = (f32[8]{0:T(128)S(1)}, f32[8]{0:T(128)}, u32[]{:S(2)}) copy-start(f32[8]{0:T(128)} %tfs_h.1) | copy-start | bytes 100
  0.0 7.5 %copy-start.5 = (f32[8]{0:T(128)S(1)}, f32[8]{0:T(128)}, u32[]{:S(2)}) copy-start(f32[8]{0:T(128)} %tfc_h.1) | copy-start | bytes 100
  0.1 7.5 %copy-start.4 = (f32[3]{0:T(128)S(1)}, f32[3]{0:T(128)}, u32[]{:S(2)}) copy-start(f32[3]{0:T(128)} %dif_h.1) | copy-start | bytes 40

commit v8 on v7

--- a/solution.py
+++ b/solution.py
@@ -403,7 +403,8 @@
     def draw(chunk, own):
         @pl.loop(0, chips)
         def _(j):
-            k = 2 * ((chip + j + 2) % chips) + (core if own else 1 - core)
+            owner = core if own else 1 - core
+            k = 2 * ((chip + jnp.where(owner == 0, j + 2, 6 - j)) % chips) + owner
             sharp = 0.5 * tfs[k]
             out_ref = mine.at[chunk, j + (chips if own else 0)]
             render(ta, rise_d, rise_g, out_ref, sharp, -sharp * tfc[k], 0.5 * tfo[k])
@@ -420,7 +421,7 @@
     def combine(chunk):
         for j in (0, 1, 3, 2):
             swap_of(chunk, j).wait_recv()
-            i = (chip + j + 2) % chips
+            i = (chip + jnp.where(core == 0, j + 2, 6 - j)) % chips
             held = mine.at[chunk, chips + j]
             place = whole.at[chip, chunk] if j == 2 else held
             for n in range(CHUNK // 32):

time: 43.5 us -> 43.5 us (level)
  no operation moved by 1% of the time
where the time goes in v8:
time: 43.5 us; the launch traced here: 43.3 us
  Pallas kernels  41.6 us (96%)
  between operations  0.93 us (2%)
  local copies, waits for them, and re-layouts  0.83 us (2%)
    pallas_call x1, Pallas kernels, image(): pl.pallas_call(image_kernel, out_shape=jax.ShapeDtypeStruct((4, CX, CY),...  34.9 us
    pallas_call x1, Pallas kernels, deposit(): pl.pallas_call(deposit_kernel, out_shape=jax.ShapeDtypeStruct((CZ, PLANE,...  6.62 us

profile of v8, /device:TPU:6, one launch (start us, length us, event | category | flops | bytes accessed | tf_op | source)
XLA Modules:
  0.0 43.3 jit_solution(667331106552470355)
XLA Ops:
  0.0 0.0 copy-start.2
  0.0 0.0 copy-start.1
  0.0 0.0 copy-start
  0.0 0.0 copy-start.3
  0.0 0.0 copy-start.8
  0.0 0.0 copy-start.7
  0.0 0.0 copy-start.6
  0.0 0.0 copy-start.5
  0.1 0.0 copy-start.4
  0.9 6.6 %deposit.1.ext = f32[16,288,128]{2,1,0:T(8,128)S(1)} custom-call(s32[1,1]{1,0:T(1,128)S(6)} %copy.17.count, s32[128,128]{1,0:T(8,128)} %bitcast.5, s32[128,128]{1,0:T(8,128)} %bitcast.6, s32[128,128]{1,0:T(8,128)} %bitcast.7, bf16[1,1,16384]{2,1,0:T(2,128)(2,1)} %mh.1, bf16[256,256]{1,0:T(8,128)(2,1)} %constant.8.clone.fh), custom_call_target="tpu_custom_call" | custom-call | tf_op jit(solution)/shard_map/deposit/pallas_call | solution.py:180
  7.5 0.0 copy-done.2
  7.5 0.0 copy-done.1
  7.5 0.0 copy-done
  7.5 0.0 copy-done.3
  7.5 0.0 copy-done.8
  7.5 0.0 copy-done.7
  7.5 0.0 copy-done.6
  7.6 0.0 copy-done.5
  7.6 0.0 copy-done.4
  7.6 34.9 %image.1 = f32[4,256,128]{2,1,0:T(8,128)S(1)} custom-call(f32[3]{0:T(128)S(1)} %copy-done.4, f32[8]{0:T(128)S(1)} %copy-done.5, f32[8]{0:T(128)S(1)} %copy-done.6, f32[8]{0:T(128)S(1)} %copy-done.7, f32[8]{0:T(128)S(1)} %copy-done.8, f32[3,8]{1,0:T(4,128)S(1)} %bitcast.4, f32[8,128]{1,0:T(8,128)S(1)} %copy-done.2, bf16[256,256]{1,0:T(8,128)(2,1)S(1)} %copy-done, ...), custom_call_target="tpu_custom_call" | custom-call | tf_op jit(solution)/shard_map/image/pallas_call | solution.py:505
  42.5 0.8 %copy.18 = f32[4,256,128]{2,1,0:T(8,128)} copy(f32[4,256,128]{2,1,0:T(8,128)S(1)} %image.1) | data formatting | bytes 1048576
Async XLA Ops:
  0.0 7.5 %copy-start.2 = (f32[8,128]{1,0:T(8,128)S(1)}, f32[8,128]{1,0:T(8,128)}, u32[]{:S(2)}) copy-start(f32[8,128]{1,0:T(8,128)} %constant.11.clone.cosine_h) | copy-start | bytes 12292
  0.0 7.5 %copy-start.1 = (bf16[128,256]{1,0:T(8,128)(2,1)S(1)}, bf16[128,256]{1,0:T(8,128)(2,1)}, u32[]{:S(2)}) copy-start(bf16[128,256]{1,0:T(8,128)(2,1)} %constant.10.clone.low_h) | copy-start | bytes 196612
  0.0 7.5 %copy-start = (bf16[256,256]{1,0:T(8,128)(2,1)S(1)}, bf16[256,256]{1,0:T(8,128)(2,1)}, u32[]{:S(2)}) copy-start(bf16[256,256]{1,0:T(8,128)(2,1)} %constant.9.clone.back_h) | copy-start | bytes 393220
  0.0 7.5 %copy-start.3 = (f32[8,3]{0,1:T(4,128)S(1)}, f32[8,3]{0,1:T(4,128)}, u32[]{:S(2)}) copy-start(f32[8,3]{0,1:T(4,128)} %param.25) | copy-start | bytes 292
  0.0 7.5 %copy-start.8 = (f32[8]{0:T(128)S(1)}, f32[8]{0:T(128)}, u32[]{:S(2)}) copy-start(f32[8]{0:T(128)} %shade_h.1) | copy-start | bytes 100
  0.0 7.5 %copy-start.7 = (f32[8]{0:T(128)S(1)}, f32[8]{0:T(128)}, u32[]{:S(2)}) copy-start(f32[8]{0:T(128)} %tfo_h.1) | copy-start | bytes 100
  0.0 7.5 %copy-start.6 = (f32[8]{0:T(128)S(1)}, f32[8]{0:T(128)}, u32[]{:S(2)}) copy-start(f32[8]{0:T(128)} %tfs_h.1) | copy-start | bytes 100
  0.0 7.5 %copy-start.5 = (f32[8]{0:T(128)S(1)}, f32[8]{0:T(128)}, u32[]{:S(2)}) copy-start(f32[8]{0:T(128)} %tfc_h.1) | copy-start | bytes 100
  0.1 7.5 %copy-start.4 = (f32[3]{0:T(128)S(1)}, f32[3]{0:T(128)}, u32[]{:S(2)}) copy-start(f32[3]{0:T(128)} %dif_h.1) | copy-start | bytes 40
